TPU v7x, 128 devices: a whole 4x4x4 slice. The times are simulated.
128 devices in a mesh: section: 8 (over x, core), space: 16 (over z, y).
Axes of the slice: x: 4, y: 4, z: 4, core: 2. Of those that a mesh axis runs over, the one named last changes fastest.
Arguments:
- volume: bfloat16 [8, 32, 8, 8, 64], P('section', 'space'), may hold values from -6 to 6
- w_first: bfloat16 [1728, 128], replicated, may hold values from -0.25 to 0.25
- w_enc: bfloat16 [3456, 128], replicated, may hold values from -0.1875 to 0.1875
- w_down: bfloat16 [1024, 256], replicated, may hold values from -0.25 to 0.25
- w_bottom: bfloat16 [6912, 256], replicated, may hold values from -0.125 to 0.125
- w_up: bfloat16 [256, 1024], replicated, may hold values from -0.375 to 0.375
- w_join: bfloat16 [6912, 128], replicated, may hold values from -0.125 to 0.125
- cotangent: bfloat16 [8, 32, 8, 8, 128], P('section', 'space'), may hold values from -6 to 6
Outputs:
- decoded: bfloat16 [8, 32, 8, 8, 128], P('section', 'space')
- grad_first: float32 [1728, 128], P(None, 'space')
- grad_enc: float32 [3456, 128], P(None, 'space')
- grad_down: float32 [1024, 256], P(None, 'space')
- grad_bottom: float32 [6912, 256], P(None, 'space')
- grad_up: float32 [256, 1024], P(None, 'space')
- grad_join: float32 [6912, 128], P(None, 'space')
All inputs are finite; a program needn't handle non-finite values.
Results may differ from a plain program's by a relative error of at most 0.025.
Values may be sent and summed in bfloat16 or wider, within the bound.
A program may use at most 128 MiB of HBM per device.

v0:
```python
import math

import jax
import jax.numpy as jnp
from jax import lax
from jax.sharding import PartitionSpec as P


def padded_2(array, sides, width):
    for axis, dim in sides:
        devices, length = (lax.axis_size(axis), array.shape[dim])
        up = [(i, (i + 1) % devices) for i in range(devices - 1)]
        down = [(j, i) for i, j in up]
        last = lax.slice_in_dim(array, length - width, length, axis=dim)
        leading = lax.slice_in_dim(array, 0, width, axis=dim)
        before = lax.ppermute(last, axis, up)
        after = lax.ppermute(leading, axis, down)
        array = jnp.concatenate([before, array, after], axis=dim)
    return array


def in_blocks(array, dim, devices):
    shape = array.shape
    parts = array.reshape(*shape[:dim], devices, shape[dim] // devices, *shape[dim + 1 :])
    return jnp.moveaxis(parts, dim, 0)


def one_scatter(arrays, axis, dims):
    devices = lax.axis_size(axis)
    parts = [in_blocks(a, dim, devices) for a, dim in zip(arrays, dims)]
    lines = jnp.concatenate([b.reshape(devices, -1) for b in parts], axis=1)
    rows = max(16, -(-lines.shape[1] // 1024) * 8)
    lines = jnp.pad(lines, ((0, 0), (0, rows * 128 - lines.shape[1]))).reshape(-1, 128)
    vector, at, finished = (lax.psum_scatter(lines, axis, tiled=True).reshape(-1), 0, [])
    for b in parts:
        part = b[0]
        finished.append(vector[at : at + part.size].reshape(part.shape))
        at += part.size
    return tuple(finished)


def sent_to_all(array, axis):
    copies = jnp.broadcast_to(array, (lax.axis_size(axis), *array.shape))
    return lax.all_to_all(copies, axis, split_axis=0, concat_axis=0, tiled=True)


def of_everyone(array, axis):
    return sent_to_all(array, axis).astype(jnp.float32).sum(axis=0)


def sent_together(arrays, axis, dim, along):
    both = jnp.concatenate(arrays, axis=along)
    result, at, finished = (lax.psum_scatter(both, axis, scatter_dimension=dim, tiled=True), 0, [])
    for a in arrays:
        finished.append(lax.slice_in_dim(result, at, at + a.shape[along], axis=along))
        at += a.shape[along]
    return tuple(finished)


def pad_sides(rimmed):
    return jnp.pad(rimmed, ((0, 0), (1, 1), (1, 1), (0, 0)))


def fine_rims(field):
    return pad_sides(padded_2(field, (("space", 0),), 1))


def coarse_rims(field):
    return pad_sides(padded_2(field, (("space", 0),), 1))


def silu_slope(pre):
    logistic = jax.nn.sigmoid(pre)
    return logistic * (1.0 + pre * (1.0 - logistic))


def to_blocks(field):
    size_x, size_y, size_z, width = field.shape
    blocks = field.reshape(size_x // 2, 2, size_y // 2, 2, size_z // 2, 2, width).transpose(
        0, 2, 4, 1, 3, 5, 6
    )
    return blocks.reshape(-1, 8 * width)


def from_blocks(flat, coarse, width):
    size_x, size_y, size_z = coarse
    spread = flat.reshape(size_x, size_y, size_z, 2, 2, 2, width).transpose(0, 3, 1, 4, 2, 5, 6)
    return spread.reshape(2 * size_x, 2 * size_y, 2 * size_z, width)


def convolve(padded, weight, extent):
    size_x, size_y, size_z = extent
    width_in = padded.shape[-1]
    summed = jnp.zeros((size_x * size_y * size_z, weight.shape[-1]), jnp.float32)
    for across in range(3):
        for upward in range(3):
            for inward in range(3):
                tap_index = across * 9 + upward * 3 + inward
                window_part = padded[
                    across : across + size_x, upward : upward + size_y, inward : inward + size_z
                ].reshape(-1, width_in)
                summed = summed + jnp.dot(
                    window_part,
                    weight[tap_index * width_in : (tap_index + 1) * width_in],
                    preferred_element_type=jnp.float32,
                )
    return summed.reshape(size_x, size_y, size_z, -1)


def transpose_conv(padded_grad, weight, extent):
    size_x, size_y, size_z = extent
    width_out = padded_grad.shape[-1]
    width_in = weight.shape[0] // 27
    summed = jnp.zeros((size_x * size_y * size_z, width_in), jnp.float32)
    for across in range(3):
        for upward in range(3):
            for inward in range(3):
                tap_index = across * 9 + upward * 3 + inward
                window_part = padded_grad[
                    2 - across : 2 - across + size_x,
                    2 - upward : 2 - upward + size_y,
                    2 - inward : 2 - inward + size_z,
                ].reshape(-1, width_out)
                block = weight[tap_index * width_in : (tap_index + 1) * width_in]
                summed = summed + lax.dot_general(
                    window_part, block, (((1,), (1,)), ((), ())), preferred_element_type=jnp.float32
                )
    return summed.reshape(size_x, size_y, size_z, width_in)


def weight_grad(padded_in, grad_pre, extent):
    size_x, size_y, size_z = extent
    width_in = padded_in.shape[-1]
    flat_grad = grad_pre.reshape(-1, grad_pre.shape[-1])
    blocks = []
    for across in range(3):
        for upward in range(3):
            for inward in range(3):
                window_part = padded_in[
                    across : across + size_x, upward : upward + size_y, inward : inward + size_z
                ].reshape(-1, width_in)
                blocks.append(
                    lax.dot_general(
                        window_part,
                        flat_grad,
                        (((0,), (0,)), ((), ())),
                        preferred_element_type=jnp.float32,
                    )
                )
    return jnp.concatenate(blocks, 0)


def activate(pre):
    return jax.nn.silu(pre).astype(jnp.bfloat16)


def pulled(grad_in, pre):
    return (grad_in.astype(jnp.float32) * silu_slope(pre)).astype(jnp.bfloat16)


def body(volume, w_first, w_enc, w_down, w_bottom, w_up, w_join, cotangent):
    section_count = lax.axis_size("section")
    space_count = lax.axis_size("space")
    field = volume[0]
    grad_out = cotangent[0]
    fine = field.shape[:3]
    coarse = (fine[0] // 2, fine[1] // 2, fine[2] // 2)
    width = w_enc.shape[1]
    wide = w_bottom.shape[1]
    pad_volume = fine_rims(field)
    pre_first = convolve(pad_volume, w_first, fine)
    act_first = activate(pre_first)
    pad_first = fine_rims(act_first)
    pre_enc = convolve(pad_first, w_enc, fine)
    skip_map = activate(pre_enc)
    skip_blocks = to_blocks(skip_map)
    pre_down = jnp.dot(skip_blocks, w_down, preferred_element_type=jnp.float32).reshape(
        coarse + (wide,)
    )
    act_down = activate(pre_down)
    pad_down = coarse_rims(act_down)
    pre_bottom = convolve(pad_down, w_bottom, coarse)
    act_bottom = activate(pre_bottom)
    bottom_flat = act_bottom.reshape(-1, wide)
    lifted = from_blocks(
        jnp.dot(bottom_flat, w_up, preferred_element_type=jnp.float32), coarse, width
    ).astype(jnp.bfloat16)
    joined = jnp.concatenate([lifted, skip_map], axis=-1)
    pad_joined = fine_rims(joined)
    pre_join = convolve(pad_joined, w_join, fine)
    decoded_map = activate(pre_join)
    step_join = pulled(grad_out, pre_join)
    grad_join = weight_grad(pad_joined, step_join, fine)
    back_pair = transpose_conv(fine_rims(step_join), w_join, fine)
    grad_lift = back_pair[..., :width].astype(jnp.bfloat16)
    grad_skip = back_pair[..., width:]
    lift_blocks = to_blocks(grad_lift)
    grad_up = lax.dot_general(
        bottom_flat, lift_blocks, (((0,), (0,)), ((), ())), preferred_element_type=jnp.float32
    )
    back_bottom = lax.dot_general(
        lift_blocks, w_up, (((1,), (1,)), ((), ())), preferred_element_type=jnp.float32
    )
    back_bottom = back_bottom.reshape(coarse + (wide,)).astype(jnp.bfloat16)
    part_up, part_join = tuple(
        (
            part.astype(jnp.float32)
            for part in one_scatter(
                (grad_up.astype(jnp.bfloat16), grad_join.astype(jnp.bfloat16)), "space", (1, 1)
            )
        )
    )
    sum_up, sum_join = (
        of_everyone(part_up.astype(jnp.bfloat16), "section").astype(jnp.float32),
        of_everyone(part_join.astype(jnp.bfloat16), "section").astype(jnp.float32),
    )
    step_bottom = pulled(back_bottom, pre_bottom)
    grad_bottom = weight_grad(pad_down, step_bottom, coarse)
    back_down = transpose_conv(coarse_rims(step_bottom), w_bottom, coarse).astype(jnp.bfloat16)
    step_down = pulled(back_down, pre_down).reshape(-1, wide)
    grad_down = lax.dot_general(
        skip_blocks, step_down, (((0,), (0,)), ((), ())), preferred_element_type=jnp.float32
    )
    back_skip = from_blocks(
        lax.dot_general(
            step_down, w_down, (((1,), (1,)), ((), ())), preferred_element_type=jnp.float32
        ),
        coarse,
        width,
    )
    step_enc = ((back_skip + grad_skip) * silu_slope(pre_enc)).astype(jnp.bfloat16)
    grad_enc = weight_grad(pad_first, step_enc, fine)
    back_first = transpose_conv(fine_rims(step_enc), w_enc, fine).astype(jnp.bfloat16)
    step_first = pulled(back_first, pre_first)
    grad_first = weight_grad(pad_volume, step_first, fine)
    part_first, part_enc, part_down, part_bottom = (
        *tuple(
            (
                part.astype(jnp.float32)
                for part in sent_together(
                    (grad_first.astype(jnp.bfloat16), grad_enc.astype(jnp.bfloat16)), "space", 1, 0
                )
            )
        ),
        *tuple(
            (
                part.astype(jnp.float32)
                for part in sent_together(
                    (grad_down.astype(jnp.bfloat16), grad_bottom.astype(jnp.bfloat16)),
                    "space",
                    1,
                    0,
                )
            )
        ),
    )
    sum_first, sum_enc, sum_down, sum_bottom = (
        of_everyone(part_first.astype(jnp.bfloat16), "section").astype(jnp.float32),
        of_everyone(part_enc.astype(jnp.bfloat16), "section").astype(jnp.float32),
        of_everyone(part_down.astype(jnp.bfloat16), "section").astype(jnp.float32),
        of_everyone(part_bottom.astype(jnp.bfloat16), "section").astype(jnp.float32),
    )
    factor = 1.0 / math.sqrt(section_count * space_count * fine[0] * fine[1] * fine[2])
    return (
        decoded_map[None],
        sum_first * factor,
        sum_enc * factor,
        sum_down * factor,
        sum_bottom * factor,
        sum_up * factor,
        sum_join * factor,
    )


def solution(mesh):
    return jax.shard_map(
        body,
        mesh=mesh,
        in_specs=(
            P("section", "space", None, None, None),
            P(),
            P(),
            P(),
            P(),
            P(),
            P(),
            P("section", "space", None, None, None),
        ),
        out_specs=(
            P("section", "space", None, None, None),
            P(None, "space"),
            P(None, "space"),
            P(None, "space"),
            P(None, "space"),
            P(None, "space"),
            P(None, "space"),
        ),
        check_vma=False,
    )
```

profile of v0, /device:TPU:1, one launch (start us, length us, event | category | flops | bytes accessed | tf_op | source)
XLA Modules:
  0.0 459.4 jit_solution(10301837320640952931)
XLA Ops:
  8.1 4.0 collective-permute-start
  12.1 1.3 collective-permute-start.1
  13.4 3.2 collective-permute-done.1
  21.2 3.2 collective-permute-start.2
  24.4 1.3 collective-permute-start.3
  26.0 2.9 collective-permute-done.3
  34.6 4.9 %collective-permute-start.4 = (bf16[1,4,4,256]{3,2,1,0:T(4,128)(2,1)S(1)}, bf16[1,4,4,256]{3,2,1,0:T(4,128)(2,1)S(1)}, u32[]{:S(2)}, u32[]{:S(2)}) collective-permute-start(bf16[1,4,4,256]{3,2,1,0:T(4,128)(2,1)S(1)} %fusion.526), channel_id=1, source_target_pairs={{0,1},{1,2},{2,3},{3,4},{4,5},{5,6},{6,7},{7,8},{8,9},{9,10},{10,1... | collective-permute-start | bytes 24584 | tf_op jit(solution)/shard_map/ppermute | solution.py:16
  39.4 1.3 collective-permute-start.5
  40.8 3.0 collective-permute-done.5
  73.1 4.0 collective-permute-start.6
  77.2 1.3 collective-permute-start.7
  79.7 2.4 collective-permute-done.7
  88.6 4.4 collective-permute-start.8
  93.0 1.3 collective-permute-start.9
  94.3 1.4 dot_general.1208
  95.7 1.5 copy.223
  104.2 1.2 copy-done.6
  105.4 12.4 %copy.250 = bf16[16,6912,8]{0,2,1:T(8,128)(2,1)} copy(bf16[16,6912,8]{1,0,2:T(8,128)(2,1)} %bitcast.1543) | data formatting | bytes 3538944 | tf_op jit(solution)/shard_map/transpose | solution.py:25
  117.7 11.4 %copy.251 = bf16[16,55296]{1,0:T(8,128)(2,1)} copy(bf16[16,55296]{0,1:T(8,128)(2,1)} %bitcast.1538) | data formatting | bytes 3538944 | tf_op jit(solution)/shard_map/reshape | solution.py:31
  136.4 4.0 collective-permute-start.10
  140.4 1.5 collective-permute-start.11
  142.9 1.6 reshape.1341
  144.6 1.7 pad_maximum_fusion
  146.3 2.1 reshape.1343
  153.2 1.1 convolution_add_fusion.142
  154.2 1.1 convolution_add_fusion.141
  156.4 1.1 convolution_add_fusion.139
  157.5 1.1 convolution_add_fusion.138
  158.6 1.1 convolution_add_fusion.137
  159.7 1.1 convolution_add_fusion.136
  160.8 1.1 convolution_add_fusion.135
  161.9 1.1 convolution_add_fusion.134
  163.0 1.1 convolution_add_fusion.133
  164.1 1.1 convolution_add_fusion.132
  165.2 1.1 convolution_add_fusion.131
  166.2 1.1 convolution_add_fusion.130
  167.3 1.1 convolution_add_fusion.129
  168.4 1.1 convolution_add_fusion.128
  169.5 1.1 convolution_add_fusion.127
  170.6 1.1 convolution_add_fusion.126
  171.7 1.1 convolution_add_fusion.125
  172.8 1.1 convolution_add_fusion.124
  177.2 1.1 fusion.238
  178.2 1.2 fusion
  188.7 4.1 collective-permute-start.12
  192.8 1.3 collective-permute-start.13
  195.0 2.3 collective-permute-done.13
  229.2 6.4 %copy.367 = bf16[7936,256]{0,1:T(8,128)(2,1)} copy(bf16[7936,256]{1,0:T(8,128)(2,1)} %fusion.28) | data formatting | bytes 8126464
  237.5 91.0 %all-reduce.12.cloned.1.call-done = (bf16[5184,128]{1,0:T(8,128)(2,1)}, bf16[8960,128]{1,0:T(8,128)(2,1)}) async-done(((bf16[5184,128]{1,0:T(8,128)(2,1)}, bf16[8960,128]{1,0:T(8,128)(2,1)}), (bf16[5184,128]{1,0:T(8,128)(2,1)}, bf16[8960,128]{1,0:T(8,128)(2,1)})) %all-reduce.12.cloned.1.call-update) | async-done | bytes 3620880
  328.6 1.3 constant_dynamic-slice_fusion.1
  330.8 5.6 %all-to-all-start = ((bf16[8,1728,8]{1,2,0:T(8,128)(2,1)}), bf16[8,1728,8]{1,2,0:T(8,128)(2,1)S(1)}, u32[]{:S(2)}, u32[]{:S(2)}) async-start(bf16[8,1728,8]{1,2,0:T(8,128)(2,1)} %broadcast_in_dim.19), calls=%async_computation | async-start | bytes 458752 | tf_op jit(solution)/shard_map/all_to_all | solution.py:44
  337.9 4.6 all-to-all-done
  343.2 4.3 all-to-all-start.4
  348.2 5.8 %all-to-all-done.4 = bf16[8,256,64]{1,2,0:T(8,128)(2,1)S(1)} async-done(((bf16[8,256,64]{1,2,0:T(8,128)(2,1)}), bf16[8,256,64]{1,2,0:T(8,128)(2,1)S(1)}, u32[]{:S(2)}, u32[]{:S(2)}) %all-to-all-start.4) | async-done | bytes 262176 | tf_op jit(solution)/shard_map/all_to_all | solution.py:44
  354.8 4.4 all-to-all-start.1
  360.8 1.9 reshape.1345
  363.5 4.2 all-to-all-done.1
  368.7 4.4 all-to-all-start.5
  374.5 33.7 %reduce-scatter.5.cloned.1.call-done = bf16[16,7936]{1,0:T(8,128)(2,1)} async-done(((bf16[256,7936]{1,0:T(8,128)(2,1)}), bf16[16,7936]{1,0:T(8,128)(2,1)}) %reduce-scatter.5.cloned.1.call-update) | async-done | bytes 253968
  409.7 6.7 %all-to-all-start.2 = ((bf16[8,1024,16]{1,2,0:T(8,128)(2,1)}), bf16[8,1024,16]{1,2,0:T(8,128)(2,1)S(1)}, u32[]{:S(2)}, u32[]{:S(2)}) async-start(bf16[8,1024,16]{1,2,0:T(8,128)(2,1)} %broadcast_in_dim.21), calls=%async_computation.2 | async-start | bytes 524288 | tf_op jit(solution)/shard_map/all_to_all | solution.py:44
  417.3 5.7 %all-to-all-done.2 = bf16[8,1024,16]{1,2,0:T(8,128)(2,1)S(1)} async-done(((bf16[8,1024,16]{1,2,0:T(8,128)(2,1)}), bf16[8,1024,16]{1,2,0:T(8,128)(2,1)S(1)}, u32[]{:S(2)}, u32[]{:S(2)}) %all-to-all-start.2) | async-done | bytes 262176 | tf_op jit(solution)/shard_map/all_to_all | solution.py:44
  422.9 1.3 broadcast_in_dim.22
  424.3 4.5 all-to-all-start.3
  430.2 21.3 %all-to-all-done.3 = bf16[8,6912,16]{1,2,0:T(8,128)(2,1)S(1)} async-done(((bf16[8,6912,16]{1,2,0:T(8,128)(2,1)}), bf16[8,6912,16]{1,2,0:T(8,128)(2,1)S(1)}, u32[]{:S(2)}, u32[]{:S(2)}) %all-to-all-start.3) | async-done | bytes 1769504 | tf_op jit(solution)/shard_map/all_to_all | solution.py:44
  (530 shorter events, 128.0 us)
Async XLA Ops:
  7.2 27.1 %copy-start = (bf16[1024,256]{1,0:T(8,128)(2,1)S(1)}, bf16[1024,256]{1,0:T(8,128)(2,1)}, u32[]{:S(2)}) copy-start(bf16[1024,256]{1,0:T(8,128)(2,1)} %param.11) | copy-start | bytes 1572868
  7.2 11.2 %copy-start.9 = (bf16[1,2,8,8,64]{4,3,2,1,0:T(8,128)(2,1)S(1)}, bf16[1,2,8,8,64]{4,3,2,1,0:T(8,128)(2,1)}, u32[]{:S(2)}) copy-start(bf16[1,2,8,8,64]{4,3,2,1,0:T(8,128)(2,1)} %param.8) | copy-start | bytes 49156
  7.2 10.4 %copy-start.15 = (bf16[1728,128]{1,0:T(8,128)(2,1)S(1)}, bf16[1728,128]{1,0:T(8,128)(2,1)}, u32[]{:S(2)}) copy-start(bf16[1728,128]{1,0:T(8,128)(2,1)} %param.9) | copy-start | bytes 1327108
  7.2 321.4 %all-reduce.12.cloned.1.call-start = ((), (), s32[]{:S(2)}) async-start(), calls=%async_computation.8 | async-start | bytes 7241728
  8.1 5.3 %collective-permute-start = (bf16[1,8,8,64]{3,2,1,0:T(8,128)(2,1)S(1)}, bf16[1,8,8,64]{3,2,1,0:T(8,128)(2,1)S(1)}, u32[]{:S(2)}, u32[]{:S(2)}) collective-permute-start(bf16[1,8,8,64]{3,2,1,0:T(8,128)(2,1)S(1)} %get-tuple-element.195), channel_id=1, source_target_pairs={{0,1},{1,2},{2,3},{3,4},{4,5},{5,6},{6,7},{7,8},{8,9},{9,10},{10,1... | collective-permute-start | bytes 24584 | tf_op jit(solution)/shard_map/ppermute | solution.py:16
  12.1 4.5 collective-permute-start.1
  13.4 5.5 %copy-start.31 = (bf16[1,8,8,64]{3,2,1,0:T(8,128)(2,1)}, bf16[1,8,8,64]{3,2,1,0:T(8,128)(2,1)S(1)}, u32[]{:S(2)}) copy-start(bf16[1,8,8,64]{3,2,1,0:T(8,128)(2,1)S(1)} %collective-permute-done) | copy-start | bytes 24580
  16.6 2.3 copy-start.29
  18.8 7.0 %copy-start.4 = (bf16[256,1024]{1,0:T(8,128)(2,1)S(1)}, bf16[256,1024]{1,0:T(8,128)(2,1)}, u32[]{:S(2)}) copy-start(bf16[256,1024]{1,0:T(8,128)(2,1)} %param.13) | copy-start | bytes 1572868
  20.8 9.0 %copy-start.2 = (bf16[3456,128]{1,0:T(8,128)(2,1)S(1)}, bf16[3456,128]{1,0:T(8,128)(2,1)}, u32[]{:S(2)}) copy-start(bf16[3456,128]{1,0:T(8,128)(2,1)} %param.10) | copy-start | bytes 2654212
  21.2 9.2 %copy-start.13 = (bf16[2,8,8,128]{3,2,1,0:T(8,128)(2,1)}, bf16[2,8,8,128]{3,2,1,0:T(8,128)(2,1)S(1)}, u32[]{:S(2)}) copy-start(bf16[2,8,8,128]{3,2,1,0:T(8,128)(2,1)S(1)} %multiply_convert_fusion.6) | copy-start | bytes 98308
  21.2 4.7 %collective-permute-start.2 = (bf16[1,8,8,128]{3,2,1,0:T(8,128)(2,1)S(1)}, bf16[1,8,8,128]{3,2,1,0:T(8,128)(2,1)S(1)}, u32[]{:S(2)}, u32[]{:S(2)}) collective-permute-start(bf16[1,8,8,128]{3,2,1,0:T(8,128)(2,1)S(1)} %get-tuple-element.191), channel_id=1, source_target_pairs={{0,1},{1,2},{2,3},{3,4},{4,5},{5,6},{6,7},{7,8},{8,9},{9,10},{10,1... | collective-permute-start | bytes 49160 | tf_op jit(solution)/shard_map/ppermute | solution.py:16
  24.4 4.5 collective-permute-start.3
  26.0 3.0 copy-start.36
  34.3 23.5 %copy-start.27 = (bf16[16,1024]{1,0:T(8,128)(2,1)}, bf16[16,1024]{1,0:T(8,128)(2,1)S(1)}, u32[]{:S(2)}) copy-start(bf16[16,1024]{1,0:T(8,128)(2,1)S(1)} %reshape.1169) | copy-start | bytes 98308
  34.5 44.0 %copy-start.21 = (f32[16,256]{1,0:T(8,128)}, f32[16,256]{1,0:T(8,128)S(1)}, u32[]{:S(2)}) copy-start(f32[16,256]{1,0:T(8,128)S(1)} %fusion.682) | copy-start | bytes 49156
  34.6 6.2 %collective-permute-start.4 = (bf16[1,4,4,256]{3,2,1,0:T(4,128)(2,1)S(1)}, bf16[1,4,4,256]{3,2,1,0:T(4,128)(2,1)S(1)}, u32[]{:S(2)}, u32[]{:S(2)}) collective-permute-start(bf16[1,4,4,256]{3,2,1,0:T(4,128)(2,1)S(1)} %fusion.526), channel_id=1, source_target_pairs={{0,1},{1,2},{2,3},{3,4},{4,5},{5,6},{6,7},{7,8},{8,9},{9,10},{10,1... | collective-permute-start | bytes 24584 | tf_op jit(solution)/shard_map/ppermute | solution.py:16
  39.4 4.4 collective-permute-start.5
  40.8 20.4 %copy-start.42 = (bf16[1,4,4,256]{3,2,1,0:T(4,128)(2,1)}, bf16[1,4,4,256]{3,2,1,0:T(4,128)(2,1)S(1)}, u32[]{:S(2)}) copy-start(bf16[1,4,4,256]{3,2,1,0:T(4,128)(2,1)S(1)} %collective-permute-done.4) | copy-start | bytes 24580
  43.8 24.7 %copy-start.40 = (bf16[1,4,4,256]{3,2,1,0:T(4,128)(2,1)}, bf16[1,4,4,256]{3,2,1,0:T(4,128)(2,1)S(1)}, u32[]{:S(2)}) copy-start(bf16[1,4,4,256]{3,2,1,0:T(4,128)(2,1)S(1)} %collective-permute-done.5) | copy-start | bytes 24580
  73.1 6.6 %collective-permute-start.6 = (bf16[1,8,8,256]{3,2,1,0:T(8,128)(2,1)S(1)}, bf16[1,8,8,256]{3,2,1,0:T(8,128)(2,1)S(1)}, u32[]{:S(2)}, u32[]{:S(2)}) collective-permute-start(bf16[1,8,8,256]{3,2,1,0:T(8,128)(2,1)S(1)} %get-tuple-element.179), channel_id=1, source_target_pairs={{0,1},{1,2},{2,3},{3,4},{4,5},{5,6},{6,7},{7,8},{8,9},{9,10},{10,1... | collective-permute-start | bytes 98312 | tf_op jit(solution)/shard_map/ppermute | solution.py:16
  77.2 4.9 %collective-permute-start.7 = (bf16[1,8,8,256]{3,2,1,0:T(8,128)(2,1)S(1)}, bf16[1,8,8,256]{3,2,1,0:T(8,128)(2,1)S(1)}, u32[]{:S(2)}, u32[]{:S(2)}) collective-permute-start(bf16[1,8,8,256]{3,2,1,0:T(8,128)(2,1)S(1)} %get-tuple-element.180), channel_id=1, source_target_pairs={{1,0},{2,1},{3,2},{4,3},{5,4},{6,5},{7,6},{8,7},{9,8},{10,9},{11,1... | collective-permute-start | bytes 98312 | tf_op jit(solution)/shard_map/ppermute | solution.py:17
  79.7 3.3 copy-start.1
  79.7 2.4 copy-start.23
  82.9 1.1 copy-start.24
  83.3 1.9 copy-start.45
  84.0 2.2 copy-start.12
  84.0 2.7 copy-start.10
  85.1 2.0 copy-start.44
  87.9 6.3 %copy-start.18 = (f32[128,128]{1,0:T(8,128)}, f32[128,128]{1,0:T(8,128)S(1)}, u32[]{:S(2)}) copy-start(f32[128,128]{1,0:T(8,128)S(1)} %get-tuple-element.202) | copy-start | bytes 196612
  88.6 40.5 %collective-permute-start.8 = (bf16[1,8,8,128]{3,2,1,0:T(8,128)(2,1)}, bf16[1,8,8,128]{3,2,1,0:T(8,128)(2,1)}, u32[]{:S(2)}, u32[]{:S(2)}) collective-permute-start(bf16[1,8,8,128]{3,2,1,0:T(8,128)(2,1)} %get-tuple-element.187), channel_id=1, source_target_pairs={{0,1},{1,2},{2,3},{3,4},{4,5},{5,6},{6,7},{7,8},{8,9},{9,10},{10,1... | collective-permute-start | bytes 49160 | tf_op jit(solution)/shard_map/ppermute | solution.py:16
  93.0 36.2 %collective-permute-start.9 = (bf16[1,8,8,128]{3,2,1,0:T(8,128)(2,1)}, bf16[1,8,8,128]{3,2,1,0:T(8,128)(2,1)}, u32[]{:S(2)}, u32[]{:S(2)}) collective-permute-start(bf16[1,8,8,128]{3,2,1,0:T(8,128)(2,1)} %get-tuple-element.188), channel_id=1, source_target_pairs={{1,0},{2,1},{3,2},{4,3},{5,4},{6,5},{7,6},{8,7},{9,8},{10,9},{11,1... | collective-permute-start | bytes 49160 | tf_op jit(solution)/shard_map/ppermute | solution.py:17
  101.0 2.1 copy-start.11
  104.2 1.2 copy-start.6
  130.9 2.3 copy-start.46
  133.9 2.3 copy-start.5
  133.9 2.2 copy-start.39
  136.4 12.0 %collective-permute-start.10 = (bf16[1,4,4,256]{3,2,1,0:T(4,128)(2,1)S(1)}, bf16[1,4,4,256]{3,2,1,0:T(4,128)(2,1)S(1)}, u32[]{:S(2)}, u32[]{:S(2)}) collective-permute-start(bf16[1,4,4,256]{3,2,1,0:T(4,128)(2,1)S(1)} %bitcast.1698), channel_id=1, source_target_pairs={{0,1},{1,2},{2,3},{3,4},{4,5},{5,6},{6,7},{7,8},{8,9},{9,10},{10,1... | collective-permute-start | bytes 24584 | tf_op jit(solution)/shard_map/ppermute | solution.py:16
  140.4 8.0 %collective-permute-start.11 = (bf16[1,4,4,256]{3,2,1,0:T(4,128)(2,1)S(1)}, bf16[1,4,4,256]{3,2,1,0:T(4,128)(2,1)S(1)}, u32[]{:S(2)}, u32[]{:S(2)}) collective-permute-start(bf16[1,4,4,256]{3,2,1,0:T(4,128)(2,1)S(1)} %bitcast.1699), channel_id=1, source_target_pairs={{1,0},{2,1},{3,2},{4,3},{5,4},{6,5},{7,6},{8,7},{9,8},{10,9},{11,1... | collective-permute-start | bytes 24584 | tf_op jit(solution)/shard_map/ppermute | solution.py:17
  155.3 21.8 %copy-start.22 = (f32[16,256]{1,0:T(8,128)S(1)}, f32[16,256]{1,0:T(8,128)}, u32[]{:S(2)}) copy-start(f32[16,256]{1,0:T(8,128)} %copy-done.21) | copy-start | bytes 49156
  156.4 21.8 %copy-start.28 = (bf16[16,1024]{1,0:T(8,128)(2,1)S(1)}, bf16[16,1024]{1,0:T(8,128)(2,1)}, u32[]{:S(2)}) copy-start(bf16[16,1024]{1,0:T(8,128)(2,1)} %copy-done.27) | copy-start | bytes 98308
  170.6 12.4 %copy-start.43 = (bf16[1,4,4,256]{3,2,1,0:T(4,128)(2,1)S(1)}, bf16[1,4,4,256]{3,2,1,0:T(4,128)(2,1)}, u32[]{:S(2)}) copy-start(bf16[1,4,4,256]{3,2,1,0:T(4,128)(2,1)} %copy-done.42) | copy-start | bytes 24580
  181.2 7.4 %copy-start.17 = (f32[128,256]{1,0:T(8,128)S(1)}, f32[128,256]{1,0:T(8,128)}, u32[]{:S(2)}) copy-start(f32[128,256]{1,0:T(8,128)} %copy-done.16) | copy-start | bytes 393220
  187.4 10.0 %copy-start.3 = (bf16[3456,128]{1,0:T(8,128)(2,1)S(1)}, bf16[3456,128]{1,0:T(8,128)(2,1)}, u32[]{:S(2)}) copy-start(bf16[3456,128]{1,0:T(8,128)(2,1)} %param.10) | copy-start | bytes 2654212
  188.7 6.3 %collective-permute-start.12 = (bf16[1,8,8,128]{3,2,1,0:T(8,128)(2,1)S(1)}, bf16[1,8,8,128]{3,2,1,0:T(8,128)(2,1)S(1)}, u32[]{:S(2)}, u32[]{:S(2)}) collective-permute-start(bf16[1,8,8,128]{3,2,1,0:T(8,128)(2,1)S(1)} %get-tuple-element.183), channel_id=1, source_target_pairs={{0,1},{1,2},{2,3},{3,4},{4,5},{5,6},{6,7},{7,8},{8,9},{9,10},{10,1... | collective-permute-start | bytes 49160 | tf_op jit(solution)/shard_map/ppermute | solution.py:16
  192.8 4.5 collective-permute-start.13
  200.0 2.6 copy-start.32
  203.0 3.4 copy-start.30
  206.0 2.4 copy-start.14
  206.0 2.4 copy-start.38
  210.8 1.9 copy-start.35
  213.8 1.1 copy-start.8
  213.9 2.9 copy-start.47
  215.0 193.2 %reduce-scatter.5.cloned.1.call-start = ((), (), s32[]{:S(2)}) async-start(), calls=%async_computation.7 | async-start | bytes 4317184
  216.8 8.0 %copy-start.41 = (bf16[1,4,4,256]{3,2,1,0:T(4,128)(2,1)S(1)}, bf16[1,4,4,256]{3,2,1,0:T(4,128)(2,1)}, u32[]{:S(2)}) copy-start(bf16[1,4,4,256]{3,2,1,0:T(4,128)(2,1)} %copy-done.40) | copy-start | bytes 24580
  328.6 19.0 %copy-start.7 = (bf16[5184,128]{1,0:T(8,128)(2,1)S(1)}, bf16[5184,128]{1,0:T(8,128)(2,1)}, u32[]{:S(2)}) copy-start(bf16[5184,128]{1,0:T(8,128)(2,1)} %get-tuple-element.7) | copy-start | bytes 3981316
  330.8 11.7 %all-to-all-start = ((bf16[8,1728,8]{1,2,0:T(8,128)(2,1)}), bf16[8,1728,8]{1,2,0:T(8,128)(2,1)S(1)}, u32[]{:S(2)}, u32[]{:S(2)}) async-start(bf16[8,1728,8]{1,2,0:T(8,128)(2,1)} %broadcast_in_dim.19), calls=%async_computation | async-start | bytes 458752 | tf_op jit(solution)/shard_map/all_to_all | solution.py:44
  343.2 10.8 %all-to-all-start.4 = ((bf16[8,256,64]{1,2,0:T(8,128)(2,1)}), bf16[8,256,64]{1,2,0:T(8,128)(2,1)S(1)}, u32[]{:S(2)}, u32[]{:S(2)}) async-start(bf16[8,256,64]{1,2,0:T(8,128)(2,1)} %broadcast_in_dim.23), calls=%async_computation.4 | async-start | bytes 524288 | tf_op jit(solution)/shard_map/all_to_all | solution.py:44
  347.5 11.7 %copy-start.19 = (f32[128,128]{1,0:T(8,128)S(1)}, f32[128,128]{1,0:T(8,128)}, u32[]{:S(2)}) copy-start(f32[128,128]{1,0:T(8,128)} %copy-done.18) | copy-start | bytes 196612
  354.8 12.9 %all-to-all-start.1 = ((bf16[8,3456,8]{1,2,0:T(8,128)(2,1)}), bf16[8,3456,8]{1,2,0:T(8,128)(2,1)S(1)}, u32[]{:S(2)}, u32[]{:S(2)}) async-start(bf16[8,3456,8]{1,2,0:T(8,128)(2,1)} %broadcast_in_dim.20), calls=%async_computation.1 | async-start | bytes 884736 | tf_op jit(solution)/shard_map/all_to_all | solution.py:44
  368.7 40.3 %all-to-all-start.5 = ((bf16[8,6912,8]{1,2,0:T(8,128)(2,1)}), bf16[8,6912,8]{1,2,0:T(8,128)(2,1)S(1)}, u32[]{:S(2)}, u32[]{:S(2)}) async-start(bf16[8,6912,8]{1,2,0:T(8,128)(2,1)} %broadcast_in_dim.24), calls=%async_computation.5 | async-start | bytes 1769472 | tf_op jit(solution)/shard_map/all_to_all | solution.py:44
  408.2 9.1 %copy-start.20 = (bf16[16,7936]{1,0:T(8,128)(2,1)S(1)}, bf16[16,7936]{1,0:T(8,128)(2,1)}, u32[]{:S(2)}) copy-start(bf16[16,7936]{1,0:T(8,128)(2,1)} %reduce-scatter.5.cloned.1.call-done) | copy-start | bytes 761860
  409.7 13.2 %all-to-all-start.2 = ((bf16[8,1024,16]{1,2,0:T(8,128)(2,1)}), bf16[8,1024,16]{1,2,0:T(8,128)(2,1)S(1)}, u32[]{:S(2)}, u32[]{:S(2)}) async-start(bf16[8,1024,16]{1,2,0:T(8,128)(2,1)} %broadcast_in_dim.21), calls=%async_computation.2 | async-start | bytes 524288 | tf_op jit(solution)/shard_map/all_to_all | solution.py:44
  424.3 27.3 %all-to-all-start.3 = ((bf16[8,6912,16]{1,2,0:T(8,128)(2,1)}), bf16[8,6912,16]{1,2,0:T(8,128)(2,1)S(1)}, u32[]{:S(2)}, u32[]{:S(2)}) async-start(bf16[8,6912,16]{1,2,0:T(8,128)(2,1)} %broadcast_in_dim.22), calls=%async_computation.3 | async-start | bytes 3538944 | tf_op jit(solution)/shard_map/all_to_all | solution.py:44
  (7 other events, 5.4 us)
Sparse Core Ops, SparseCore 0:
  215.1 113.4 all-reduce.11
  331.9 76.2 reduce-scatter.4
where the time goes:
time: 463 us; the launch traced here: 459 us
  waiting for transfers between devices  180 us (39%)
  matrix products  124 us (27%)
  starting transfers between devices  67.8 us (15%)
  local copies, waits for them, and re-layouts  60.6 us (13%)
  between operations  17.3 us (4%)
  other arithmetic  9.97 us (2%)
    unnamed x4, waiting for transfers between devices  125 us
    dot_general x108, matrix products, weight_grad(): lax.dot_general(window_part, flat_grad, (((0,), (0,)), ((), ())), preferr...  42.5 us
    all_to_all x6, waiting for transfers between devices, sent_to_all(): return lax.all_to_all(copies, axis, split_axis=0, concat_axis=0, tiled=True)  41.6 us
    dot_general x108, matrix products, convolve(): jnp.dot(window_part, weight[tap_index * width_in:(tap_index + 1) * width_...  40.9 us
    dot_general x81, matrix products, transpose_conv(): lax.dot_general(window_part, block, (((1,), (1,)), ((), ())), preferred_e...  37.8 us
    all_to_all x6, starting transfers between devices, sent_to_all(): return lax.all_to_all(copies, axis, split_axis=0, concat_axis=0, tiled=True)  30 us
    ppermute x7, starting transfers between devices, padded_2(): before = lax.ppermute(last, axis, up)  28.5 us
    ppermute x7, waiting for transfers between devices, padded_2(): after = lax.ppermute(leading, axis, down)  13.8 us
  transfers between devices with their start and end apart: 22, of which 12 were waited for; matrix products, arithmetic and copies ran while one was open for 17% of the time, Pallas kernels for 0%

commit v1 on v0

v1 whole, which is shorter than its diff:
```python
import math

import jax
import jax.numpy as jnp
from jax import lax
from jax.experimental import pallas as pl
from jax.experimental.pallas import tpu as pltpu
from jax.sharding import PartitionSpec as P

BF = jnp.bfloat16
F32 = jnp.float32
MESH = pl.DeviceIdType.MESH
T = 128
GROUPS = ((0, 32), (32, 64), (96, 24), (120, 8))
JOIN_AT, UP_AT, BOTTOM_AT, DOWN_AT, ENC_AT, FIRST_AT = 0, 32, 40, 96, 104, 120
PADS = ((27, 32), (94, 96), (118, 120), (127, 128))
COLS = 128 * T
HALF, EIGHTH = COLS // 2, COLS // 8


def mm(a, b):
    return jnp.dot(a, b, preferred_element_type=F32)


def mm_t(a, b):
    return lax.dot_general(a, b, (((1,), (1,)), ((), ())), preferred_element_type=F32)


def silu(z):
    return z * jax.nn.sigmoid(z)


def slope(z):
    s = jax.nn.sigmoid(z)
    return s * (1.0 + z * (1.0 - s))


def one_hot(cond):
    return jnp.where(cond, 1.0, 0.0).astype(BF)


def iotas(shape):
    return lax.broadcasted_iota(jnp.int32, shape, 0), lax.broadcasted_iota(jnp.int32, shape, 1)


def block_row(v):
    y, z = (v >> 3) & 7, v & 7
    return ((v >> 6) * 4 + (y & 1) * 2 + (z & 1)) * 16 + (y >> 1) * 4 + (z >> 1)


def ds(at, size):
    return pl.ds(pl.multiple_of(at, T), size)


def kernel(
    vol_h, wf_h, we_h, wd_h, wb_h, wu_h, wj_h, cot_h,
    dec_o, gf_o, ge_o, gd_o, gb_o, gu_o, gj_o,
    vol, wf, we, wd, wb, wu, wj, cot, load_sem,
    shift, shift_c, perm, perm_t, eye, half_mask,
    a_f, a_e, a_j, a_s, a_b, b_b, blocks, diag,
    z1, z2, e_skip,
    h1, sk, li, t7, t2, g1, t4,
    hv, hr, hc, h_send, h_recv,
    packed, r0, u0, r1, u1, r2, u2, r3, u3, full,
    s0, q0, s1, q1, s2, q2, s3, q3, s4, q4,
):
    sec, me = lax.axis_index("section"), lax.axis_index("space")
    core, my_x = sec % 2, sec // 2
    my_z, my_y = me // 4, me % 4

    loads = []
    for i, (src, dst) in enumerate(
        ((vol_h, vol), (wf_h, wf.at[pl.ds(0, 1728)]), (we_h, we), (wd_h, wd), (wb_h, wb), (wu_h, wu), (cot_h, cot), (wj_h, wj))
    ):
        copy = pltpu.make_async_copy(src, dst, load_sem.at[i])
        copy.start()
        loads.append(copy)
    l_vol, l_wf, l_we, l_wd, l_wb, l_wu, l_cot, l_wj = loads

    after, before = (sec, (me + 1) % 16), (sec, (me + 15) % 16)
    other_core = (sec + 1 - 2 * core, me)
    y_peers = [(sec, my_z * 4 + (my_y + d) % 4) for d in (1, 2, 3)]
    z_peers = [(sec, ((my_z + d) % 4) * 4 + my_y) for d in (1, 2, 3)]
    sec_peers = [((sec + d) % 8, me) for d in range(1, 8)]

    barrier = pltpu.get_barrier_semaphore()
    peers = [after, before, *y_peers, *z_peers, *sec_peers]
    for dev in peers:
        pl.semaphore_signal(barrier, inc=1, device_id=dev, device_id_type=MESH)

    r, c = iotas((64, 64))
    for k in range(9):
        oy, oz = k // 3 - 1, k % 3 - 1
        shift[k] = one_hot(((c >> 3) == (r >> 3) + oy) & ((c & 7) == (r & 7) + oz))
    r, c = iotas((16, 16))
    for k in range(9):
        oy, oz = k // 3 - 1, k % 3 - 1
        shift_c[k * 16 : (k + 1) * 16, :] = one_hot(((c >> 2) == (r >> 2) + oy) & ((c & 3) == (r & 3) + oz))
    r, c = iotas((T, T))
    perm[...] = one_hot(r == block_row(c))
    perm_t[...] = one_hot(c == block_row(r))
    half_mask[0] = one_hot(c < 64)
    half_mask[1] = one_hot(c >= 64)
    r, c = iotas((256, 256))
    eye[...] = one_hot(r == c)
    wf[1728:1792, :] = jnp.zeros((64, T), BF)
    a_e[:, 3456:3584] = jnp.zeros((T, T), BF)
    diag[...] = jnp.zeros((T, 2048), BF)
    for lo, hi in PADS:
        packed[:, :, lo * T : hi * T] = jnp.zeros((16, 16, (hi - lo) * T), BF)

    not_first = jnp.where(me > 0, 1.0, 0.0)
    not_last = jnp.where(me < 15, 1.0, 0.0)

    sends = []

    def remote(src, dst, send_sem, recv_sem, dev):
        return pltpu.make_async_remote_copy(
            src_ref=src, dst_ref=dst, send_sem=send_sem, recv_sem=recv_sem, device_id=dev, device_id_type=MESH
        )

    def swap(index, first, last, got):
        up = remote(last, got.at[0], h_send.at[index, 0], h_recv.at[index, 0], after)
        down = remote(first, got.at[1], h_send.at[index, 1], h_recv.at[index, 1], before)
        up.start()
        down.start()
        sends.extend((up, down))
        return up, down

    def swap_fine(index, ref):
        return swap(index, ref.at[pl.ds(0, 64)], ref.at[pl.ds(64, 64)], hr.at[index])

    def arrived(pair, got):
        for copy in pair:
            copy.wait_recv()
        lo = (got[0].astype(F32) * not_first).astype(BF)
        hi = (got[1].astype(F32) * not_last).astype(BF)
        return lo, hi

    def spread(to, pair, places, stride, off):
        both = jnp.concatenate(pair, axis=1)
        for k in range(9):
            moved = mm(shift[k], both).astype(BF)
            for n, spots in enumerate(places):
                for ox, i in spots:
                    at = (ox * 9 + k) * stride + off
                    to[i * 64 : (i + 1) * 64, at : at + T] = moved[:, n * T : (n + 1) * T]

    def spread_own(to, own, stride=T, off=0):
        spread(to, (own[0:64], own[64:128]), (((1, 0), (0, 1)), ((2, 0), (1, 1))), stride, off)

    def spread_halo(to, lo, hi, stride=T, off=0):
        spread(to, (lo, hi), (((0, 0),), ((2, 1),)), stride, off)

    def spread_coarse(to, lo, own, hi):
        moved = mm(shift_c[...], jnp.concatenate([lo, own, hi], axis=1)).astype(BF)
        for ox in range(3):
            for k in range(9):
                at = (ox * 9 + k) * 256
                to[:, at : at + 256] = moved[k * 16 : (k + 1) * 16, ox * 256 : (ox + 1) * 256]

    def stacked(flat):
        return jnp.concatenate([flat[:, t * T : (t + 1) * T] for t in range(8)], axis=0)

    def grad_128(step, a, half_tiles, chunk, tile):
        step_t = mm_t(eye[0:T, 0:T], step).astype(BF)
        width = chunk * T
        for n in range(0, half_tiles, chunk):
            left = mm(step_t, a[:, n * T : n * T + width]).reshape(16, 8, width)
            right = mm(step_t, a[:, (half_tiles + n) * T : (half_tiles + n) * T + width]).reshape(16, 8, width)
            at = (tile + n) * T
            packed[:, :, at : at + width] = jnp.concatenate([left, right], axis=1).astype(BF)

    def grad_256(step, a, tiles, tile):
        step_t = mm_t(eye[...], step).astype(BF)
        for n in range(0, tiles, 2):
            at = (tile + n) * T
            packed[:, :, at : at + 256] = mm(step_t, a[:, n * T : n * T + 256]).reshape(16, 16, 256).astype(BF)

    step_1, step_2 = 1 + 3 * core, 4 - 3 * core
    at_1 = my_y + core * (my_z - my_y)
    at_2 = my_z + core * (my_y - my_z)
    flight = {}

    def peer_1(d):
        return (sec, ((at_1 + d) % 4) * step_1 + at_2 * step_2)

    def peer_2(d):
        return (sec, at_1 * step_1 + ((at_2 + d) % 4) * step_2)

    def stage_0(g):
        first, n = GROUPS[g]
        w = n // 2 * T
        copy = remote(
            packed.at[:, :, ds(first * T + (1 - core) * w, w)],
            r0.at[:, :, pl.ds(first // 2 * T, w)],
            s0.at[g], q0.at[g], other_core,
        )
        copy.start()
        flight[g] = [copy]
        sends.append(copy)

    def stage_1(g):
        first, n = GROUPS[g]
        w, at = n // 2 * T, first // 2 * T
        flight[g][0].wait_recv()
        mine = ds(first * T + core * w, w)

        def add(i, carry):
            for j in range(4):
                p = i * step_1 + j * step_2
                u0[i, j, :, at : at + w] = packed[p, :, mine] + r0[p, :, at : at + w]
            return carry

        lax.fori_loop(0, 4, add, 0)
        flight[g] = []
        for d in (1, 2, 3):
            copy = remote(
                u0.at[(at_1 + d) % 4, :, :, pl.ds(at, w)],
                r1.at[d - 1, :, :, pl.ds(at, w)],
                s1.at[g, d - 1], q1.at[g, d - 1], peer_1(d),
            )
            copy.start()
            flight[g].append(copy)
            sends.append(copy)

    def stage_2(g):
        first, n = GROUPS[g]
        w, at = n // 2 * T, first // 2 * T
        for copy in flight[g]:
            copy.wait_recv()

        def add(j, carry):
            total = u0[at_1, j, :, at : at + w].astype(F32)
            for d in range(3):
                total = total + r1[d, j, :, at : at + w].astype(F32)
            u1[j, :, at : at + w] = total.astype(BF)
            return carry

        lax.fori_loop(0, 4, add, 0)
        flight[g] = []
        for d in (1, 2, 3):
            copy = remote(
                u1.at[(at_2 + d) % 4, :, pl.ds(at, w)],
                r2.at[d - 1, :, pl.ds(at, w)],
                s2.at[g, d - 1], q2.at[g, d - 1], peer_2(d),
            )
            copy.start()
            flight[g].append(copy)
            sends.append(copy)

    def stage_3(g):
        first, n = GROUPS[g]
        w, at = n // 2 * T, first // 2 * T
        q = n // 8 * T
        for copy in flight[g]:
            copy.wait_recv()
        total = u1[at_2, :, at : at + w].astype(F32)
        for d in range(3):
            total = total + r2[d, :, at : at + w].astype(F32)
        u2[:, at : at + w] = total.astype(BF)
        flight[g] = []
        for d in (1, 2, 3):
            copy = remote(
                u2.at[:, ds(at + ((my_x + d) % 4) * q, q)],
                r3.at[d - 1, :, pl.ds(first // 8 * T, q)],
                s3.at[g, d - 1], q3.at[g, d - 1], (((my_x + d) % 4) * 2 + core, me),
            )
            copy.start()
            flight[g].append(copy)
            sends.append(copy)

    def stage_4(g):
        first, n = GROUPS[g]
        at = first // 2 * T
        q, fine_at = n // 8 * T, first // 8 * T
        for copy in flight[g]:
            copy.wait_recv()
        total = u2[:, ds(at + my_x * q, q)].astype(F32)
        for d in range(3):
            total = total + r3[d, :, fine_at : fine_at + q].astype(F32)
        done = total.astype(BF)
        u3[:, fine_at : fine_at + q] = done
        flight[g] = []
        for d in range(1, 8):
            place = first * T + core * (n // 2 * T) + my_x * q
            copy = remote(
                u3.at[:, pl.ds(fine_at, q)], full.at[:, ds(place, q)],
                s4.at[g, d - 1], q4.at[g, d - 1], ((sec + d) % 8, me),
            )
            copy.start()
            sends.append(copy)
            src = (sec + 8 - d) % 8
            place = first * T + (src % 2) * (n // 2 * T) + (src // 2) * q
            flight[g].append(
                remote(
                    u3.at[:, pl.ds(fine_at, q)], full.at[:, ds(place, q)],
                    s4.at[g, d - 1], q4.at[g, d - 1], ((sec + d) % 8, me),
                )
            )
        full[:, ds(first * T + core * (n // 2 * T) + my_x * q, q)] = done

    def stage_5(g):
        for copy in flight[g]:
            copy.wait_recv()

    l_vol.wait()
    pl.semaphore_wait(barrier, len(peers))
    pair = swap(5, vol.at[pl.ds(0, 64)], vol.at[pl.ds(64, 64)], hv)
    r, c = iotas((64, T))
    twice = one_hot(r == (c & 63))
    h1[...] = mm(vol[...], twice).astype(BF)
    spread_own(a_s, h1)
    lo, hi = arrived(pair, hv)
    spread_halo(a_s, mm(lo, twice).astype(BF), mm(hi, twice).astype(BF))
    for j in range(14):
        tile = a_s[:, 2 * j * T : (2 * j + 1) * T] * half_mask[0]
        if j < 13:
            tile = tile + a_s[:, (2 * j + 1) * T : (2 * j + 2) * T] * half_mask[1]
        a_f[:, j * T : (j + 1) * T] = tile
    l_wf.wait()
    pre = mm(a_f[...], wf[...])
    z1[...] = pre
    h1[...] = silu(pre).astype(BF)
    pair = swap_fine(0, h1)
    spread_own(a_e, h1)
    l_we.wait()
    spread_halo(a_e, *arrived(pair, hr.at[0]))
    pre = mm(a_e[:, 0:3456], we[...])
    z2[...] = pre
    sk[...] = silu(pre).astype(BF)
    skip_pair = swap_fine(1, sk)
    moved = mm(perm[...], sk[...]).astype(BF)
    for t in range(8):
        blocks[:, t * T : (t + 1) * T] = moved[t * 16 : (t + 1) * 16]
    l_wd.wait()
    z3 = mm(blocks[...], wd[...])
    g1[...] = silu(z3).astype(BF)
    pair = swap(6, g1, g1, hc.at[0])
    spread_own(a_j, sk, 256, T)
    spread_halo(a_j, *arrived(skip_pair, hr.at[1]), 256, T)
    l_wb.wait()
    lo, hi = arrived(pair, hc.at[0])
    spread_coarse(a_b, lo, g1[...], hi)
    z4 = mm(a_b[...], wb[...])
    g2 = silu(z4).astype(BF)
    l_wu.wait()
    lifted = stacked(mm(g2, wu[...]).astype(BF))
    li[...] = mm(perm_t[...], lifted).astype(BF)
    pair = swap_fine(2, li)
    spread_own(a_j, li, 256, 0)
    l_wj.wait()
    l_cot.wait()
    spread_halo(a_j, *arrived(pair, hr.at[2]), 256, 0)
    pre = mm(a_j[...], wj[...])
    dec_o[...] = silu(pre).astype(BF)

    t7[...] = (cot[...].astype(F32) * slope(pre)).astype(BF)
    pair = swap_fine(3, t7)
    grad_128(t7[...], a_j, 27, 3, JOIN_AT)
    stage_0(0)
    spread_own(a_s, t7)
    spread_halo(a_s, *arrived(pair, hr.at[3]))
    back = jnp.zeros((T, 256), F32)
    for tap in range(27):
        back = back + mm_t(a_s[:, (26 - tap) * T : (27 - tap) * T], wj[tap * 256 : (tap + 1) * 256, :])
    e_skip[...] = back[:, T:256]
    moved = mm(perm[...], back[:, 0:T].astype(BF)).astype(BF)
    lift_blocks = jnp.concatenate([moved[t * 16 : (t + 1) * 16] for t in range(8)], axis=1)
    e3 = mm_t(lift_blocks, wu[...]).astype(BF)
    t4[...] = (e3.astype(F32) * slope(z4)).astype(BF)
    pair = swap(7, t4, t4, hc.at[1])
    stage_1(0)
    for t in range(8):
        diag[t * 16 : (t + 1) * 16, t * 256 : (t + 1) * 256] = g2
    moved_t = mm_t(eye[0:T, 0:T], moved).astype(BF)
    for t in range(8):
        up = mm(moved_t, diag[:, t * 256 : (t + 1) * 256]).astype(BF)
        for b in range(8):
            at = UP_AT * T + (b % 4) * 256
            packed[2 * t + b // 4, :, at : at + 256] = up[b * 16 : (b + 1) * 16]
    grad_256(t4[...], a_b, 54, BOTTOM_AT)
    stage_0(1)
    lo, hi = arrived(pair, hc.at[1])
    spread_coarse(b_b, lo, t4[...], hi)
    back = jnp.zeros((16, 256), F32)
    for tap in range(27):
        back = back + mm_t(b_b[:, (26 - tap) * 256 : (27 - tap) * 256], wb[tap * 256 : (tap + 1) * 256, :])
    e4 = back.astype(BF)
    t3 = (e4.astype(F32) * slope(z3)).astype(BF)
    e5 = stacked(mm_t(t3, wd[...]))
    high = e5.astype(BF)
    low = (e5 - high.astype(F32)).astype(BF)
    e5 = mm(perm_t[...], high) + mm(perm_t[...], low)
    t2[...] = ((e5 + e_skip[...]) * slope(z2[...])).astype(BF)
    pair = swap_fine(4, t2)
    stage_1(1)
    grad_256(t3, blocks, 8, DOWN_AT)
    grad_128(t2[...], a_e, 14, 2, ENC_AT)
    stage_0(2)
    stage_2(0)
    spread_own(a_s, t2)
    spread_halo(a_s, *arrived(pair, hr.at[4]))
    back = jnp.zeros((T, T), F32)
    for tap in range(27):
        back = back + mm_t(a_s[:, (26 - tap) * T : (27 - tap) * T], we[tap * T : (tap + 1) * T, :])
    t1 = (back.astype(BF).astype(F32) * slope(z1[...])).astype(BF)
    stage_1(2)
    grad_128(t1, a_f, 7, 1, FIRST_AT)
    stage_0(3)
    stage_3(0)
    stage_1(3)
    stage_4(0)
    stage_2(1)
    stage_2(2)
    stage_2(3)
    stage_3(1)
    stage_3(2)
    stage_3(3)
    stage_4(1)
    stage_4(2)
    stage_4(3)

    factor = 1.0 / math.sqrt(16384)

    def rows(tile, width):
        return full[:, tile * T : tile * T + width].astype(F32) * factor

    stage_5(0)
    both = rows(JOIN_AT, 3456)
    gj_o[:, 0:3456] = both[0:8]
    gj_o[:, 3456:6912] = both[8:16]
    stage_5(1)
    for b in range(4):
        gu_o[b * 16 : (b + 1) * 16, :] = rows(UP_AT + 2 * b, 256)
    gb_o[...] = rows(BOTTOM_AT, 6912)
    stage_5(2)
    gd_o[...] = rows(DOWN_AT, 1024)
    both = rows(ENC_AT, 1792)
    ge_o[:, 0:1792] = both[0:8]
    ge_o[:, 1792:3456] = both[8:16, 0:1664]
    stage_5(3)
    both = rows(FIRST_AT, 896)
    gf_o[:, 0:896] = both[0:8]
    gf_o[:, 896:1728] = both[8:16, 0:832]
    for copy in sends:
        copy.wait_send()


def scratch():
    v, dma = pltpu.VMEM, pltpu.SemaphoreType.DMA
    return [
        v((128, 64), BF), v((1792, 128), BF), v((3456, 128), BF), v((1024, 256), BF), v((6912, 256), BF),
        v((256, 1024), BF), v((6912, 128), BF), v((128, 128), BF), dma((8,)),
        v((9, 64, 64), BF), v((144, 16), BF), v((T, T), BF), v((T, T), BF), v((256, 256), BF), v((2, T, T), BF),
        v((T, 1792), BF), v((T, 3584), BF), v((T, 6912), BF), v((T, 3456), BF), v((16, 6912), BF), v((16, 6912), BF),
        v((16, 1024), BF), v((T, 2048), BF),
        v((T, T), F32), v((T, T), F32), v((T, T), F32),
        v((T, T), BF), v((T, T), BF), v((T, T), BF), v((T, T), BF), v((T, T), BF), v((16, 256), BF), v((16, 256), BF),
        v((2, 64, 64), BF), v((5, 2, 64, T), BF), v((2, 2, 16, 256), BF), dma((8, 2)), dma((8, 2)),
        v((16, 16, COLS), BF), v((16, 16, HALF), BF), v((4, 4, 16, HALF), BF), v((3, 4, 16, HALF), BF),
        v((4, 16, HALF), BF), v((3, 16, HALF), BF), v((16, HALF), BF), v((3, 16, EIGHTH), BF), v((16, EIGHTH), BF),
        v((16, COLS), BF),
        dma((4,)), dma((4,)), dma((4, 3)), dma((4, 3)), dma((4, 3)), dma((4, 3)), dma((4, 3)), dma((4, 3)),
        dma((4, 7)), dma((4, 7)),
    ]


def body(volume, w_first, w_enc, w_down, w_bottom, w_up, w_join, cotangent):
    out = lambda shape, dtype=F32: jax.ShapeDtypeStruct(shape, dtype)
    results = pl.pallas_call(
        kernel,
        out_shape=(
            out((128, 128), BF), out((8, 1728)), out((8, 3456)), out((16, 1024)), out((16, 6912)), out((64, 256)),
            out((8, 6912)),
        ),
        in_specs=[pl.BlockSpec(memory_space=pl.ANY)] * 8,
        out_specs=[pl.BlockSpec(memory_space=pltpu.VMEM)] * 7,
        scratch_shapes=scratch(),
        compiler_params=pltpu.CompilerParams(
            collective_id=0, has_side_effects=True, vmem_limit_bytes=58 * 1024 * 1024
        ),
        name="step",
    )(
        volume.reshape(128, 64), w_first, w_enc, w_down, w_bottom, w_up, w_join, cotangent.reshape(128, 128)
    )
    decoded, *grads = results
    return (decoded.reshape(1, 2, 8, 8, 128), *(g.T for g in grads))


def solution(mesh):
    crops = P("section", "space", None, None, None)
    return jax.shard_map(
        body,
        mesh=mesh,
        in_specs=(crops, P(), P(), P(), P(), P(), P(), crops),
        out_specs=(crops, *([P(None, "space")] * 6)),
        check_vma=False,
    )
```

time: 463 us -> 93.9 us (0.20)
  waiting for transfers between devices: 180 us -> 0 us
  matrix products: 124 us -> 0 us
  Pallas kernels: 0 us -> 82.1 us
  starting transfers between devices: 67.8 us -> 0 us
  local copies, waits for them, and re-layouts: 60.6 us -> 10.7 us
  between operations: 17.3 us -> 0.65 us
  other arithmetic: 9.97 us -> 0 us
    unnamed x4 -> x0, waiting for transfers between devices: 125 us -> none
    dot_general x303 -> x0, matrix products: 124 us -> none  [the longest x108 42.5 us: weight_grad(): lax.dot_general(window_part, flat_grad, (((0,), (0,)), ((), ())), preferr...]
    pallas_call x0 -> x1, Pallas kernels: none -> 82.1 us  [body(): pl.pallas_call(kernel, out_shape=(out((128, 128), BF), out((8, 1728)), ou...]
    all_to_all x6 -> x0, waiting for transfers between devices: 41.6 us -> none  [sent_to_all(): return lax.all_to_all(copies, axis, split_axis=0, concat_axis=0, tiled=True)]
    ppermute x14 -> x0, starting transfers between devices: 37.8 us -> none  [the longest x7 28.5 us: padded_2(): before = lax.ppermute(last, axis, up)]
    all_to_all x6 -> x0, starting transfers between devices: 30 us -> none  [sent_to_all(): return lax.all_to_all(copies, axis, split_axis=0, concat_axis=0, tiled=True)]
    reshape x66 -> x0, local copies, waits for them, and re-layouts: 19.9 us -> none  [the longest x2 13 us: one_scatter(): lines = jnp.concatenate([b.reshape(devices, -1) for b in parts], axis=1)]
    ppermute x14 -> x0, waiting for transfers between devices: 13.9 us -> none  [the longest x7 13.8 us: padded_2(): after = lax.ppermute(leading, axis, down)]
  transfers between devices with their start and end apart: 22 -> 0, of which waited for: 12 -> 0; matrix products, arithmetic and copies ran while one was open for 17% -> 0% of each run, Pallas kernels for 0% -> 0%
where the time goes in v1:
time: 93.9 us; the launch traced here: 93.5 us
  Pallas kernels  82.1 us (87%)
  local copies, waits for them, and re-layouts  10.7 us (11%)
    pallas_call x1, Pallas kernels, body(): pl.pallas_call(kernel, out_shape=(out((128, 128), BF), out((8, 1728)), ou...  82.1 us
    unnamed x7, local copies, waits for them, and re-layouts  10.7 us

profile of v1, /device:TPU:1, one launch (start us, length us, event | category | flops | bytes accessed | tf_op | source)
XLA Modules:
  0.0 93.5 jit_solution(12467124779736586754)
XLA Ops:
  0.6 82.1 %step.1 = (bf16[128,128]{1,0:T(8,128)(2,1)}, f32[8,1728]{1,0:T(8,128)}, f32[8,3456]{1,0:T(8,128)}, f32[16,1024]{1,0:T(8,128)}, f32[16,6912]{1,0:T(8,128)}, /*index=5*/f32[64,256]{1,0:T(8,128)}, f32[8,6912]{1,0:T(8,128)}) custom-call(bf16[128,64]{1,0:T(8,128)(2,1)} %bitcast.15, bf16[1728,128]{1,0:T(8,128)(2,1)} %wf_h.1, bf16[3456,128]{1,0:T(8,128)(2,1)} %we_h.1, ...), custom_call_target="tpu_custom_call" | custom-call | tf_op jit(solution)/shard_map/step/pallas_call | solution.py:471
  82.7 1.4 %copy.22 = bf16[1,2,8,8,128]{4,3,2,1,0:T(8,128)(2,1)} copy(bf16[1,2,8,8,128]{4,3,2,1,0:T(8,128)(2,1)} %bitcast.17) | data formatting | bytes 65536
  84.1 1.4 %copy.23 = f32[1728,8]{0,1:T(8,128)} copy(f32[1728,8]{0,1:T(8,128)} %bitcast.14) | data formatting | bytes 110592
  85.6 1.5 %copy.24 = f32[3456,8]{0,1:T(8,128)} copy(f32[3456,8]{0,1:T(8,128)} %bitcast.11) | data formatting | bytes 221184
  87.1 1.5 %copy.25 = f32[1024,16]{0,1:T(8,128)} copy(f32[1024,16]{0,1:T(8,128)} %bitcast.13) | data formatting | bytes 131072
  88.6 1.8 %copy.26 = f32[6912,16]{0,1:T(8,128)} copy(f32[6912,16]{0,1:T(8,128)} %bitcast.9) | data formatting | bytes 884736
  90.4 1.5 %copy.27 = f32[256,64]{0,1:T(8,128)} copy(f32[256,64]{0,1:T(8,128)} %bitcast.12) | data formatting | bytes 131072
  91.8 1.6 %copy.28 = f32[6912,8]{0,1:T(8,128)} copy(f32[6912,8]{0,1:T(8,128)} %bitcast.10) | data formatting | bytes 442368

commit v2 on v1

v2 whole, which is shorter than its diff:
```python
import math

import jax
import jax.numpy as jnp
from jax import lax
from jax.experimental import pallas as pl
from jax.experimental.pallas import tpu as pltpu
from jax.sharding import PartitionSpec as P

BF = jnp.bfloat16
F32 = jnp.float32
MESH = pl.DeviceIdType.MESH
T = 128
GROUPS = ((0, 32), (32, 64), (96, 24), (120, 8))
JOIN_AT, UP_AT, BOTTOM_AT, DOWN_AT, ENC_AT, FIRST_AT = 0, 32, 40, 96, 104, 120
PADS = ((27, 32), (94, 96), (118, 120), (127, 128))
COLS = 128 * T
HALF, EIGHTH = COLS // 2, COLS // 8


def mm(a, b):
    return jnp.dot(a, b, preferred_element_type=F32)


def mm_t(a, b):
    return lax.dot_general(a, b, (((1,), (1,)), ((), ())), preferred_element_type=F32)


def silu(z):
    return z * jax.nn.sigmoid(z)


def slope(z):
    s = jax.nn.sigmoid(z)
    return s * (1.0 + z * (1.0 - s))


def one_hot(cond):
    return jnp.where(cond, 1.0, 0.0).astype(BF)


def iotas(shape):
    return lax.broadcasted_iota(jnp.int32, shape, 0), lax.broadcasted_iota(jnp.int32, shape, 1)


def block_row(v):
    y, z = (v >> 3) & 7, v & 7
    return ((v >> 6) * 4 + (y & 1) * 2 + (z & 1)) * 16 + (y >> 1) * 4 + (z >> 1)


def ds(at, size):
    return pl.ds(pl.multiple_of(at, T), size)


def kernel(
    vol_h, wf_h, we_h, wd_h, wb_h, wu_h, wj_h, cot_h,
    dec_o, full_o,
    vol, wf, we, wd, wb, wu, wj, cot, load_sem,
    shift, shift_c, perm, perm_t, eye, half_mask,
    wx, b_v, b_1, b_j, b_s, b_c, b_4, a_f, blocks, diag,
    z1, z2, e_skip,
    h1, sk, li, t7, t2, t4,
    h_vol, h_cot, h_t2, h_t4, h_send, h_recv,
    packed, r0, u0, r1, u1, r2, u2, r3, u3, full,
    s0, q0, s1, q1, s2, q2, s3, q3, s4, q4,
):
    sec, me = lax.axis_index("section"), lax.axis_index("space")
    core, my_x = sec % 2, sec // 2
    my_z, my_y = me // 4, me % 4

    loads = []
    for i, (src, dst) in enumerate(
        ((vol_h, vol), (wf_h, wf), (we_h, we), (wd_h, wd), (wb_h, wb), (wu_h, wu), (cot_h, cot), (wj_h, wj))
    ):
        copy = pltpu.make_async_copy(src, dst, load_sem.at[i])
        copy.start()
        loads.append(copy)
    l_vol, l_wf, l_we, l_wd, l_wb, l_wu, l_cot, l_wj = loads

    around = {d: (sec, (me + 16 + d) % 16) for d in (-3, -2, -1, 1, 2, 3)}
    after, before = around[1], around[-1]
    other_core = (sec + 1 - 2 * core, me)
    y_peers = [(sec, my_z * 4 + (my_y + d) % 4) for d in (1, 2, 3)]
    z_peers = [(sec, ((my_z + d) % 4) * 4 + my_y) for d in (1, 2, 3)]
    sec_peers = [((sec + d) % 8, me) for d in range(1, 8)]

    barrier = pltpu.get_barrier_semaphore()
    peers = [*around.values(), *y_peers, *z_peers, *sec_peers]
    for dev in peers:
        pl.semaphore_signal(barrier, inc=1, device_id=dev, device_id_type=MESH)

    r, c = iotas((64, 64))
    for k in range(9):
        oy, oz = k // 3 - 1, k % 3 - 1
        shift[k] = one_hot(((c >> 3) == (r >> 3) + oy) & ((c & 7) == (r & 7) + oz))
    r, c = iotas((16, 16))
    for k in range(9):
        oy, oz = k // 3 - 1, k % 3 - 1
        shift_c[k * 16 : (k + 1) * 16, :] = one_hot(((c >> 2) == (r >> 2) + oy) & ((c & 3) == (r & 3) + oz))
    r, c = iotas((T, T))
    perm[...] = one_hot(r == block_row(c))
    perm_t[...] = one_hot(c == block_row(r))
    half_mask[0] = one_hot(c < 64)
    half_mask[1] = one_hot(c >= 64)
    r, c = iotas((256, 256))
    eye[...] = one_hot(r == c)
    diag[...] = jnp.zeros((T, 2048), BF)
    for lo, hi in PADS:
        packed[:, :, lo * T : hi * T] = jnp.zeros((16, 16, (hi - lo) * T), BF)

    not_first = jnp.where(me > 0, 1.0, 0.0)
    not_last = jnp.where(me < 15, 1.0, 0.0)

    sends = []

    def remote(src, dst, send_sem, recv_sem, dev):
        return pltpu.make_async_remote_copy(
            src_ref=src, dst_ref=dst, send_sem=send_sem, recv_sem=recv_sem, device_id=dev, device_id_type=MESH
        )

    def push(index, src, dst, dev):
        copy = remote(src, dst, h_send.at[index], h_recv.at[index], dev)
        copy.start()
        sends.append(copy)
        return copy

    def swap(index, first, last, got):
        return push(index, last, got.at[0], after), push(index + 1, first, got.at[1], before)

    def arrived(pair, got):
        for copy in pair:
            copy.wait_recv()
        lo = (got[0].astype(F32) * not_first).astype(BF)
        hi = (got[1].astype(F32) * not_last).astype(BF)
        return lo, hi

    def inside(x, first, count, layer_rows):
        layer = lax.broadcasted_iota(jnp.int32, x.shape, 0) // layer_rows + first
        return jnp.where((layer >= 0) & (layer < count), x, 0.0).astype(BF)

    def spread(to, layers, row=0, per=2, width=T):
        step = per * 64 // 64
        for n in range(0, len(layers), step):
            group = layers[n : n + step]
            both = jnp.concatenate(group, axis=1)
            for k in range(9):
                moved = mm(shift[k], both).astype(BF)
                for m in range(len(group)):
                    to[row + (n + m) * 64 : row + (n + m + 1) * 64, k * width : (k + 1) * width] = (
                        moved[:, m * width : (m + 1) * width]
                    )

    def layers_of(x):
        return [x[i : i + 64] for i in range(0, x.shape[0], 64)]

    def spread_coarse(to, layers):
        moved = mm(shift_c[...], jnp.concatenate(layers, axis=1)).astype(BF)
        for n in range(len(layers)):
            for k in range(9):
                to[n * 16 : (n + 1) * 16, k * 256 : (k + 1) * 256] = (
                    moved[k * 16 : (k + 1) * 16, n * 256 : (n + 1) * 256]
                )

    def conv(b, w, count, rows):
        depth = b.shape[1]
        total = mm(b[0:count], w[0:depth, :])
        for ox in (1, 2):
            total = total + mm(b[ox * rows : ox * rows + count], w[ox * depth : (ox + 1) * depth, :])
        return total

    def conv_back(b, w, count, rows):
        cols = b.shape[1] // 9
        depth = w.shape[0] // 27
        total = jnp.zeros((count, depth), F32)
        for ox in range(3):
            for k in range(9):
                tap = ox * 9 + k
                total = total + mm_t(
                    b[(2 - ox) * rows : (2 - ox) * rows + count, (8 - k) * cols : (9 - k) * cols],
                    w[tap * depth : (tap + 1) * depth, :],
                )
        return total

    def stacked(flat):
        return jnp.concatenate([flat[:, t * T : (t + 1) * T] for t in range(8)], axis=0)

    def grad_128(step_t, part, tiles, half, chunk, tile):
        width = chunk * T

        def piece(n):
            if n >= tiles:
                return jnp.zeros((16, 8, width), F32)
            return mm(step_t, part(n)).reshape(16, 8, width)

        for n in range(0, half, chunk):
            at = (tile + n) * T
            packed[:, :, at : at + width] = jnp.concatenate([piece(n), piece(half + n)], axis=1).astype(BF)

    def grad_256(step_t, part, tiles, tile):
        for n in range(0, tiles, 2):
            at = (tile + n) * T
            packed[:, :, at : at + 256] = mm(step_t, part(n)).reshape(16, 16, 256).astype(BF)

    def turned(x):
        return mm_t(eye[0 : x.shape[1], 0 : x.shape[1]], x).astype(BF)

    def window(b, at, rows, count, chunk):
        per = b.shape[1] // T

        def part(n):
            ox, k = n // per, n % per
            begin = at + ox * rows
            return b[begin : begin + count, k * T : (k + chunk) * T]

        return part

    step_1, step_2 = 1 + 3 * core, 4 - 3 * core
    at_1 = my_y + core * (my_z - my_y)
    at_2 = my_z + core * (my_y - my_z)
    flight = {}

    def peer_1(d):
        return (sec, ((at_1 + d) % 4) * step_1 + at_2 * step_2)

    def peer_2(d):
        return (sec, at_1 * step_1 + ((at_2 + d) % 4) * step_2)

    def stage_0(g):
        first, n = GROUPS[g]
        w = n // 2 * T
        copy = remote(
            packed.at[:, :, ds(first * T + (1 - core) * w, w)],
            r0.at[:, :, pl.ds(first // 2 * T, w)],
            s0.at[g], q0.at[g], other_core,
        )
        copy.start()
        flight[g] = [copy]
        sends.append(copy)

    def stage_1(g):
        first, n = GROUPS[g]
        w, at = n // 2 * T, first // 2 * T
        flight[g][0].wait_recv()
        mine = ds(first * T + core * w, w)

        def add(i, carry):
            for j in range(4):
                p = i * step_1 + j * step_2
                u0[i, j, :, at : at + w] = packed[p, :, mine] + r0[p, :, at : at + w]
            return carry

        lax.fori_loop(0, 4, add, 0)
        flight[g] = []
        for d in (1, 2, 3):
            copy = remote(
                u0.at[(at_1 + d) % 4, :, :, pl.ds(at, w)],
                r1.at[d - 1, :, :, pl.ds(at, w)],
                s1.at[g, d - 1], q1.at[g, d - 1], peer_1(d),
            )
            copy.start()
            flight[g].append(copy)
            sends.append(copy)

    def stage_2(g):
        first, n = GROUPS[g]
        w, at = n // 2 * T, first // 2 * T
        for copy in flight[g]:
            copy.wait_recv()

        def add(j, carry):
            total = u0[at_1, j, :, at : at + w].astype(F32)
            for d in range(3):
                total = total + r1[d, j, :, at : at + w].astype(F32)
            u1[j, :, at : at + w] = total.astype(BF)
            return carry

        lax.fori_loop(0, 4, add, 0)
        flight[g] = []
        for d in (1, 2, 3):
            copy = remote(
                u1.at[(at_2 + d) % 4, :, pl.ds(at, w)],
                r2.at[d - 1, :, pl.ds(at, w)],
                s2.at[g, d - 1], q2.at[g, d - 1], peer_2(d),
            )
            copy.start()
            flight[g].append(copy)
            sends.append(copy)

    def stage_3(g):
        first, n = GROUPS[g]
        w, at = n // 2 * T, first // 2 * T
        q = n // 8 * T
        for copy in flight[g]:
            copy.wait_recv()
        total = u1[at_2, :, at : at + w].astype(F32)
        for d in range(3):
            total = total + r2[d, :, at : at + w].astype(F32)
        u2[:, at : at + w] = total.astype(BF)
        flight[g] = []
        for d in (1, 2, 3):
            copy = remote(
                u2.at[:, ds(at + ((my_x + d) % 4) * q, q)],
                r3.at[d - 1, :, pl.ds(first // 8 * T, q)],
                s3.at[g, d - 1], q3.at[g, d - 1], (((my_x + d) % 4) * 2 + core, me),
            )
            copy.start()
            flight[g].append(copy)
            sends.append(copy)

    def stage_4(g):
        first, n = GROUPS[g]
        at = first // 2 * T
        q, fine_at = n // 8 * T, first // 8 * T
        for copy in flight[g]:
            copy.wait_recv()
        total = u2[:, ds(at + my_x * q, q)].astype(F32)
        for d in range(3):
            total = total + r3[d, :, fine_at : fine_at + q].astype(F32)
        done = total.astype(BF)
        u3[:, fine_at : fine_at + q] = done
        flight[g] = []
        for d in range(1, 8):
            place = first * T + core * (n // 2 * T) + my_x * q
            copy = remote(
                u3.at[:, pl.ds(fine_at, q)], full.at[:, ds(place, q)],
                s4.at[g, d - 1], q4.at[g, d - 1], ((sec + d) % 8, me),
            )
            copy.start()
            sends.append(copy)
            src = (sec + 8 - d) % 8
            place = first * T + (src % 2) * (n // 2 * T) + (src // 2) * q
            flight[g].append(
                remote(
                    u3.at[:, pl.ds(fine_at, q)], full.at[:, ds(place, q)],
                    s4.at[g, d - 1], q4.at[g, d - 1], ((sec + d) % 8, me),
                )
            )
        full[:, ds(first * T + core * (n // 2 * T) + my_x * q, q)] = done

    def stage_5(g):
        for copy in flight[g]:
            copy.wait_recv()

    l_vol.wait()
    l_cot.wait()
    pl.semaphore_wait(barrier, len(peers))
    pushed = {}
    for n, d in enumerate((1, -1, 2, -2, 3, -3)):
        pushed[-d] = push(n, vol, h_vol.at[3 - d], around[d])
    cot_pair = swap(6, cot.at[pl.ds(0, 64)], cot.at[pl.ds(64, 64)], h_cot)
    r, c = iotas((64, T))
    twice = one_hot(r == (c & 63))
    l_wf.wait()
    zero = jnp.zeros((64, T), BF)
    for tap in range(27):
        wx[tap * T : tap * T + 64, :] = wf[tap * 64 : (tap + 1) * 64, :]
        wx[tap * T + 64 : (tap + 1) * T, :] = zero
    spread(b_v, layers_of(mm(vol[...], twice).astype(BF)), 6 * 64)
    for d in (-1, 1, -2, 2, -3, 3):
        pushed[d].wait_recv()
        got = inside(mm(h_vol[3 + d], twice), 2 * (me + d), 32, 64)
        spread(b_v, layers_of(got), (3 + d) * T)
    z1_all = conv(b_v, wx, 768, 64)
    z1[...] = z1_all[320:448]
    h1[...] = inside(silu(z1_all), 2 * me - 5, 32, 64)
    spread(b_1, layers_of(h1))
    l_we.wait()
    z2_all = conv(b_1, we, 640, 64)
    z2[...] = z2_all[256:384]
    sk[...] = inside(silu(z2_all), 2 * me - 4, 32, 64)
    for n in range(5):
        moved = mm(perm[...], sk[n * T : (n + 1) * T]).astype(BF)
        for t in range(8):
            blocks[n * 16 : (n + 1) * 16, t * T : (t + 1) * T] = moved[t * 16 : (t + 1) * 16]
    l_wd.wait()
    z3 = mm(blocks[...], wd[...])
    g1 = silu(z3).astype(BF)
    spread_coarse(b_c, [g1[n * 16 : (n + 1) * 16] for n in range(5)])
    l_wb.wait()
    z4 = conv(b_c, wb, 48, 16)
    g2 = inside(silu(z4), me - 1, 16, 16)
    l_wu.wait()
    lifted = mm(g2, wu[...]).astype(BF)
    for n in range(3):
        li[n * T : (n + 1) * T] = mm(perm_t[...], stacked(lifted[n * 16 : (n + 1) * 16])).astype(BF)
    layers = [
        jnp.concatenate([li[n * 64 : (n + 1) * 64], sk[(n + 2) * 64 : (n + 3) * 64]], axis=1) for n in range(6)
    ]
    spread(b_j, layers, 0, 1, 256)
    l_wj.wait()
    z7 = conv(b_j, wj, 256, 64)
    dec_o[...] = silu(z7[64:192]).astype(BF)

    lo, hi = arrived(cot_pair, h_cot)
    cots = jnp.concatenate([lo, cot[...], hi], axis=0)
    t7[...] = (cots.astype(F32) * slope(z7)).astype(BF)
    grad_128(turned(t7[64:192]), window(b_j, 64, 64, T, 3), 54, 27, 3, JOIN_AT)
    stage_0(0)
    spread(b_s, layers_of(t7))
    back = conv_back(b_s, wj, T, 64)
    e_skip[...] = back[:, T:256]
    moved = mm(perm[...], back[:, 0:T].astype(BF)).astype(BF)
    lift_blocks = jnp.concatenate([moved[t * 16 : (t + 1) * 16] for t in range(8)], axis=1)
    e3 = mm_t(lift_blocks, wu[...]).astype(BF)
    t4[...] = (e3.astype(F32) * slope(z4[16:32])).astype(BF)
    pair = swap(8, t4, t4, h_t4)
    stage_1(0)
    for t in range(8):
        diag[t * 16 : (t + 1) * 16, t * 256 : (t + 1) * 256] = g2[16:32]
    moved_t = turned(moved)
    for t in range(8):
        up = mm(moved_t, diag[:, t * 256 : (t + 1) * 256]).astype(BF)
        for b in range(8):
            at = UP_AT * T + (b % 4) * 256
            packed[2 * t + b // 4, :, at : at + 256] = up[b * 16 : (b + 1) * 16]
    grad_256(turned(t4[...]), window(b_c, 16, 16, 16, 2), 54, BOTTOM_AT)
    stage_0(1)
    lo, hi = arrived(pair, h_t4)
    spread_coarse(b_4, [lo, t4[...], hi])
    e4 = conv_back(b_4, wb, 16, 16).astype(BF)
    t3 = (e4.astype(F32) * slope(z3[32:48])).astype(BF)
    e5 = stacked(mm_t(t3, wd[...]))
    high = e5.astype(BF)
    low = (e5 - high.astype(F32)).astype(BF)
    e5 = mm(perm_t[...], high) + mm(perm_t[...], low)
    t2[...] = ((e5 + e_skip[...]) * slope(z2[...])).astype(BF)
    pair = swap(10, t2.at[pl.ds(0, 64)], t2.at[pl.ds(64, 64)], h_t2)
    stage_1(1)
    grad_256(turned(t3), lambda n: blocks[32:48, n * T : (n + 2) * T], 8, DOWN_AT)
    grad_128(turned(t2[...]), window(b_1, 256, 64, T, 1), 27, 14, 1, ENC_AT)
    stage_0(2)
    stage_2(0)
    spread(b_s, layers_of(t2), 64)
    lo, hi = arrived(pair, h_t2)
    spread(b_s, [lo], 0)
    spread(b_s, [hi], 192)
    back = conv_back(b_s, we, T, 64)
    t1 = (back.astype(BF).astype(F32) * slope(z1[...])).astype(BF)
    stage_1(2)
    for j in range(14):
        left, right = (b_v[320 + t // 9 * 64 : 448 + t // 9 * 64, t % 9 * T : (t % 9 + 1) * T] for t in (2 * j, min(2 * j + 1, 26)))
        tile = left * half_mask[0]
        if j < 13:
            tile = tile + right * half_mask[1]
        a_f[:, j * T : (j + 1) * T] = tile
    grad_128(turned(t1), lambda n: a_f[:, n * T : (n + 1) * T], 14, 7, 1, FIRST_AT)
    stage_0(3)
    stage_3(0)
    stage_1(3)
    stage_4(0)
    stage_2(1)
    stage_2(2)
    stage_2(3)
    stage_3(1)
    stage_3(2)
    stage_3(3)
    stage_4(1)
    stage_4(2)
    stage_4(3)
    for g, (first, n) in enumerate(GROUPS):
        stage_5(g)
        full_o[:, first * T : (first + n) * T] = full[:, first * T : (first + n) * T]
    for copy in sends:
        copy.wait_send()


def finish(dec, full, dec_o, gf_o, ge_o, gd_o, gb_o, gu_o, gj_o):
    factor = 1.0 / math.sqrt(16384)
    dec_o[...] = dec[...]

    def rows(tile, width):
        return full[:, tile * T : tile * T + width].astype(F32) * factor

    both = rows(JOIN_AT, 3456)
    gj_o[:, 0:3456] = both[0:8]
    gj_o[:, 3456:6912] = both[8:16]
    for b in range(4):
        gu_o[b * 16 : (b + 1) * 16, :] = rows(UP_AT + 2 * b, 256)
    gb_o[...] = rows(BOTTOM_AT, 6912)
    gd_o[...] = rows(DOWN_AT, 1024)
    both = rows(ENC_AT, 1792)
    ge_o[:, 0:1792] = both[0:8]
    ge_o[:, 1792:3456] = both[8:16, 0:1664]
    both = rows(FIRST_AT, 896)
    gf_o[:, 0:896] = both[0:8]
    gf_o[:, 896:1728] = both[8:16, 0:832]


def scratch():
    v, dma = pltpu.VMEM, pltpu.SemaphoreType.DMA
    return [
        v((128, 64), BF), v((1728, 128), BF), v((3456, 128), BF), v((1024, 256), BF), v((6912, 256), BF),
        v((256, 1024), BF), v((6912, 128), BF), v((128, 128), BF), dma((8,)),
        v((9, 64, 64), BF), v((144, 16), BF), v((T, T), BF), v((T, T), BF), v((256, 256), BF), v((2, T, T), BF),
        v((3456, T), BF), v((896, 1152), BF), v((768, 1152), BF), v((384, 2304), BF), v((256, 1152), BF),
        v((80, 2304), BF), v((48, 2304), BF), v((T, 1792), BF), v((80, 1024), BF), v((T, 2048), BF),
        v((T, T), F32), v((T, T), F32), v((T, T), F32),
        v((768, T), BF), v((640, T), BF), v((384, T), BF), v((256, T), BF), v((T, T), BF), v((16, 256), BF),
        v((7, T, 64), BF), v((2, 64, T), BF), v((2, 64, T), BF), v((2, 16, 256), BF), dma((12,)), dma((12,)),
        v((16, 16, COLS), BF), v((16, 16, HALF), BF), v((4, 4, 16, HALF), BF), v((3, 4, 16, HALF), BF),
        v((4, 16, HALF), BF), v((3, 16, HALF), BF), v((16, HALF), BF), v((3, 16, EIGHTH), BF), v((16, EIGHTH), BF),
        v((16, COLS), BF),
        dma((4,)), dma((4,)), dma((4, 3)), dma((4, 3)), dma((4, 3)), dma((4, 3)), dma((4, 3)), dma((4, 3)),
        dma((4, 7)), dma((4, 7)),
    ]


def body(volume, w_first, w_enc, w_down, w_bottom, w_up, w_join, cotangent):
    out = lambda shape, dtype=F32: jax.ShapeDtypeStruct(shape, dtype)
    done = pl.pallas_call(
        kernel,
        out_shape=(out((128, 128), BF), out((16, COLS), BF)),
        in_specs=[pl.BlockSpec(memory_space=pl.ANY)] * 8,
        out_specs=[pl.BlockSpec(memory_space=pltpu.VMEM)] * 2,
        scratch_shapes=scratch(),
        compiler_params=pltpu.CompilerParams(
            collective_id=0, has_side_effects=True, vmem_limit_bytes=58 * 1024 * 1024
        ),
        name="step",
    )(
        volume.reshape(128, 64), w_first, w_enc, w_down, w_bottom, w_up, w_join, cotangent.reshape(128, 128)
    )
    results = pl.pallas_call(
        finish,
        out_shape=(
            out((128, 128), BF), out((8, 1728)), out((8, 3456)), out((16, 1024)), out((16, 6912)), out((64, 256)),
            out((8, 6912)),
        ),
        name="finish",
    )(*done)
    decoded, *grads = results
    return (decoded.reshape(1, 2, 8, 8, 128), *(g.T for g in grads))


def solution(mesh):
    crops = P("section", "space", None, None, None)
    return jax.shard_map(
        body,
        mesh=mesh,
        in_specs=(crops, P(), P(), P(), P(), P(), P(), crops),
        out_specs=(crops, *([P(None, "space")] * 6)),
        check_vma=False,
    )
```

time: 93.9 us -> 76 us (0.81)
  local copies, waits for them, and re-layouts: 10.7 us -> 0 us
  Pallas kernels: 82.1 us -> 75.3 us
    unnamed x7 -> x0, local copies, waits for them, and re-layouts: 10.7 us -> none
    pallas_call x1 -> x2, Pallas kernels: 82.1 us -> 75.3 us  [the longest x1 73.3 us: body(): pl.pallas_call(kernel, out_shape=(out((128, 128), BF), out((16, COLS), BF...]
where the time goes in v2:
time: 76 us; the launch traced here: 75.9 us
  Pallas kernels  75.3 us (99%)
    pallas_call x1, Pallas kernels, body(): pl.pallas_call(kernel, out_shape=(out((128, 128), BF), out((16, COLS), BF...  73.3 us
    pallas_call x1, Pallas kernels, body(): pl.pallas_call(finish, out_shape=(out((128, 128), BF), out((8, 1728)), ou...  2.01 us

profile of v2, /device:TPU:1, one launch (start us, length us, event | category | flops | bytes accessed | tf_op | source)
XLA Modules:
  0.0 75.9 jit_solution(2884226475118740688)
XLA Ops:
  0.6 73.3 %step.1 = (bf16[128,128]{1,0:T(8,128)(2,1)}, bf16[16,16384]{1,0:T(8,128)(2,1)}) custom-call(bf16[128,64]{1,0:T(8,128)(2,1)} %bitcast.9, bf16[1728,128]{1,0:T(8,128)(2,1)} %wf_h.1, bf16[3456,128]{1,0:T(8,128)(2,1)} %we_h.1, bf16[1024,256]{1,0:T(8,128)(2,1)} %wd_h.1, bf16[6912,256]{1,0:T(8,128)(2,1)} %wb_h.1, bf16[256,1024]{1,0:T(8,128)(2,1)} %wu_h.1, ...), custom_call_target="tpu_custom_call" | custom-call | tf_op jit(solution)/shard_map/step/pallas_call | solution.py:510
  73.9 2.0 %finish.1 = (bf16[128,128]{1,0:T(8,128)(2,1)}, f32[8,1728]{1,0:T(8,128)}, f32[8,3456]{1,0:T(8,128)}, f32[16,1024]{1,0:T(8,128)}, f32[16,6912]{1,0:T(8,128)}, /*index=5*/f32[64,256]{1,0:T(8,128)}, f32[8,6912]{1,0:T(8,128)}) custom-call(bf16[128,128]{1,0:T(8,128)(2,1)} %get-tuple-element.16.dec, bf16[16,16384]{1,0:T(8,128)(2,1)} %get-tuple-element.17.full), custom_call_target="tpu_custom_call" | custom-call | tf_op jit(solution)/shard_map/finish/pallas_call | solution.py:523

commit v3 on v2

--- a/solution.py
+++ b/solution.py
@@ -11,11 +11,23 @@
 F32 = jnp.float32
 MESH = pl.DeviceIdType.MESH
 T = 128
-GROUPS = ((0, 32), (32, 64), (96, 24), (120, 8))
-JOIN_AT, UP_AT, BOTTOM_AT, DOWN_AT, ENC_AT, FIRST_AT = 0, 32, 40, 96, 104, 120
-PADS = ((27, 32), (94, 96), (118, 120), (127, 128))
-COLS = 128 * T
+GROUPS = ((0, 16), (16, 16), (32, 16), (48, 16), (64, 24), (88, 24), (112, 8))
+UP_AT, BOTTOM_AT, JOIN_AT, DOWN_AT, ENC_AT, FIRST_AT = 0, 8, 62, 89, 97, 112
+PADS = ((111, 112), (119, 120))
+COLS = 120 * T
 HALF, EIGHTH = COLS // 2, COLS // 8
+FLOWS = (
+    (0, "A", 0, 2, "bbd"),
+    (1, "A", 0, 2, "bbd"),
+    (2, "X", 0, 2, "bbd"),
+    (3, "A", 0, 1, "bdd"),
+    (3, "X", 1, 1, "bdd"),
+    (4, "A", 0, 2, "bbd"),
+    (4, "X", 2, 1, "bbd"),
+    (5, "A", 0, 2, "bdd"),
+    (5, "X", 2, 1, "bdd"),
+    (6, "A", 0, 1, "bdd"),
+)
 
 
 def mm(a, b):
@@ -61,8 +73,8 @@
     z1, z2, e_skip,
     h1, sk, li, t7, t2, t4,
     h_vol, h_cot, h_t2, h_t4, h_send, h_recv,
-    packed, r0, u0, r1, u1, r2, u2, r3, u3, full,
-    s0, q0, s1, q1, s2, q2, s3, q3, s4, q4,
+    packed, r0, own, full,
+    s0, q0, s4, q4, flows,
 ):
     sec, me = lax.axis_index("section"), lax.axis_index("space")
     core, my_x = sec % 2, sec // 2
@@ -184,7 +196,7 @@
     def stacked(flat):
         return jnp.concatenate([flat[:, t * T : (t + 1) * T] for t in range(8)], axis=0)
 
-    def grad_128(step_t, part, tiles, half, chunk, tile):
+    def grad_128(step_t, part, tiles, half, chunk, tile, begin=0, end=None):
         width = chunk * T
 
         def piece(n):
@@ -192,12 +204,12 @@
                 return jnp.zeros((16, 8, width), F32)
             return mm(step_t, part(n)).reshape(16, 8, width)
 
-        for n in range(0, half, chunk):
+        for n in range(begin, end or half, chunk):
             at = (tile + n) * T
             packed[:, :, at : at + width] = jnp.concatenate([piece(n), piece(half + n)], axis=1).astype(BF)
 
-    def grad_256(step_t, part, tiles, tile):
-        for n in range(0, tiles, 2):
+    def grad_256(step_t, part, begin, end, tile):
+        for n in range(begin, end, 2):
             at = (tile + n) * T
             packed[:, :, at : at + 256] = mm(step_t, part(n)).reshape(16, 16, 256).astype(BF)
 
@@ -217,15 +229,9 @@
     step_1, step_2 = 1 + 3 * core, 4 - 3 * core
     at_1 = my_y + core * (my_z - my_y)
     at_2 = my_z + core * (my_y - my_z)
-    flight = {}
-
-    def peer_1(d):
-        return (sec, ((at_1 + d) % 4) * step_1 + at_2 * step_2)
-
-    def peer_2(d):
-        return (sec, at_1 * step_1 + ((at_2 + d) % 4) * step_2)
-
-    def stage_0(g):
+    crossing, gathering = {}, {}
+
+    def cross(g):
         first, n = GROUPS[g]
         w = n // 2 * T
         copy = remote(
@@ -234,112 +240,147 @@
             s0.at[g], q0.at[g], other_core,
         )
         copy.start()
-        flight[g] = [copy]
+        crossing[g] = copy
         sends.append(copy)
 
-    def stage_1(g):
+    def flow(f):
+        g, kind, lo, tiles, how = FLOWS[f]
+        refs = flows[f]
         first, n = GROUPS[g]
-        w, at = n // 2 * T, first // 2 * T
-        flight[g][0].wait_recv()
-        mine = ds(first * T + core * w, w)
-
-        def add(i, carry):
+        e, w = n // 8, tiles * T
+        coords = (at_1, at_2, my_x) if kind == "A" else (my_x, at_1, at_2)
+        names = "12x" if kind == "A" else "x12"
+
+        def dev(axis, v):
+            if names[axis] == "1":
+                return (sec, v * step_1 + at_2 * step_2)
+            if names[axis] == "2":
+                return (sec, at_1 * step_1 + v * step_2)
+            return (v * 2 + core, me)
+
+        def go(src, dst, sem, to):
+            copy = remote(src, dst, refs["send"].at[sem], refs["recv"].at[sem], to)
+            copy.start()
+            sends.append(copy)
+            return copy
+
+        u = refs["u"][0]
+
+        def build(i, carry):
             for j in range(4):
                 p = i * step_1 + j * step_2
-                u0[i, j, :, at : at + w] = packed[p, :, mine] + r0[p, :, at : at + w]
+                for x in range(4):
+                    at = (x * e + lo) * T
+                    there = first // 2 * T + at
+                    both = packed[p, :, ds(first * T + core * (n // 2 * T) + at, w)] + r0[p, :, there : there + w]
+                    if kind == "A":
+                        u[i, j * 4 + x] = both
+                    else:
+                        u[x, i * 4 + j] = both
             return carry
 
-        lax.fori_loop(0, 4, add, 0)
-        flight[g] = []
-        for d in (1, 2, 3):
-            copy = remote(
-                u0.at[(at_1 + d) % 4, :, :, pl.ds(at, w)],
-                r1.at[d - 1, :, :, pl.ds(at, w)],
-                s1.at[g, d - 1], q1.at[g, d - 1], peer_1(d),
+        lax.fori_loop(0, 4, build, 0)
+        for axis in range(3):
+            m_count = (16, 4, 1)[axis]
+            c, u, r = coords[axis], refs["u"][axis], refs["r"][axis]
+            sem = axis * 6
+
+            def put(m, value):
+                if axis < 2:
+                    q = m_count // 4
+                    refs["u"][axis + 1][m // q, m % q] = value
+                else:
+                    own[:, (first // 8 + lo) * T : (first // 8 + lo) * T + w] = value
+
+            if how[axis] == "d":
+                copies = [
+                    go(u.at[(c + d) % 4], r.at[d - 1], sem + d - 1, dev(axis, (c + d) % 4)) for d in (1, 2, 3)
+                ]
+                yield
+                for copy in copies:
+                    copy.wait_recv()
+                for m in range(m_count):
+                    total = u[c, m].astype(F32)
+                    for d in range(3):
+                        total = total + r[d, m].astype(F32)
+                    put(m, total.astype(BF))
+                continue
+            c1, c2, c3 = c + 1 - 2 * (c % 2), (c + 2) % 4, 3 - c
+            h = m_count // 2
+            low, high = pl.ds(0, h), pl.ds(h, h)
+            keep, passed, got = refs["keep"][axis], refs["pass"][axis], refs["got"][axis]
+            copies = [
+                go(u.at[c1, low], r.at[0, low], sem, dev(axis, c1)),
+                go(u.at[c3, high], r.at[0, high], sem + 1, dev(axis, c3)),
+                go(u.at[c2, low], r.at[1, low], sem + 2, dev(axis, c1)),
+                go(u.at[c2, high], r.at[1, high], sem + 3, dev(axis, c3)),
+            ]
+            yield
+            for copy in copies:
+                copy.wait_recv()
+            for m in range(m_count):
+                passed[m] = u[c3 if m < h else c1, m] + r[1, m]
+            copies = [
+                go(passed.at[low], got.at[low], sem + 4, dev(axis, c3)),
+                go(passed.at[high], got.at[high], sem + 5, dev(axis, c1)),
+            ]
+            for m in range(m_count):
+                keep[m] = u[c, m] + r[0, m]
+            yield
+            for copy in copies:
+                copy.wait_recv()
+            for m in range(m_count):
+                put(m, keep[m] + got[m])
+
+    running, finished = {}, set()
+
+    def go_on(*which):
+        for f in which:
+            if f not in running:
+                g = FLOWS[f][0]
+                if g in crossing:
+                    crossing.pop(g).wait_recv()
+                running[f] = flow(f)
+            if next(running[f], True):
+                finished.add(f)
+
+    def gather(g, everyone=False):
+        first, n = GROUPS[g]
+        q, at = n // 8 * T, first // 8 * T
+        assert all(f in finished for f in range(len(FLOWS)) if FLOWS[f][0] == g)
+
+        def copy_of(d, source):
+            to = (sec + d) % 8 if everyone else (sec + 2 * d) % 8
+            return remote(
+                own.at[:, pl.ds(at, q)], full.at[:, ds(place_of(source), q)],
+                s4.at[g, d - 1], q4.at[g, d - 1], (to, me),
             )
-            copy.start()
-            flight[g].append(copy)
-            sends.append(copy)
-
-    def stage_2(g):
-        first, n = GROUPS[g]
-        w, at = n // 2 * T, first // 2 * T
-        for copy in flight[g]:
-            copy.wait_recv()
-
-        def add(j, carry):
-            total = u0[at_1, j, :, at : at + w].astype(F32)
-            for d in range(3):
-                total = total + r1[d, j, :, at : at + w].astype(F32)
-            u1[j, :, at : at + w] = total.astype(BF)
-            return carry
-
-        lax.fori_loop(0, 4, add, 0)
-        flight[g] = []
-        for d in (1, 2, 3):
-            copy = remote(
-                u1.at[(at_2 + d) % 4, :, pl.ds(at, w)],
-                r2.at[d - 1, :, pl.ds(at, w)],
-                s2.at[g, d - 1], q2.at[g, d - 1], peer_2(d),
-            )
-            copy.start()
-            flight[g].append(copy)
-            sends.append(copy)
-
-    def stage_3(g):
-        first, n = GROUPS[g]
-        w, at = n // 2 * T, first // 2 * T
-        q = n // 8 * T
-        for copy in flight[g]:
-            copy.wait_recv()
-        total = u1[at_2, :, at : at + w].astype(F32)
-        for d in range(3):
-            total = total + r2[d, :, at : at + w].astype(F32)
-        u2[:, at : at + w] = total.astype(BF)
-        flight[g] = []
-        for d in (1, 2, 3):
-            copy = remote(
-                u2.at[:, ds(at + ((my_x + d) % 4) * q, q)],
-                r3.at[d - 1, :, pl.ds(first // 8 * T, q)],
-                s3.at[g, d - 1], q3.at[g, d - 1], (((my_x + d) % 4) * 2 + core, me),
-            )
-            copy.start()
-            flight[g].append(copy)
-            sends.append(copy)
-
-    def stage_4(g):
-        first, n = GROUPS[g]
-        at = first // 2 * T
-        q, fine_at = n // 8 * T, first // 8 * T
-        for copy in flight[g]:
-            copy.wait_recv()
-        total = u2[:, ds(at + my_x * q, q)].astype(F32)
-        for d in range(3):
-            total = total + r3[d, :, fine_at : fine_at + q].astype(F32)
-        done = total.astype(BF)
-        u3[:, fine_at : fine_at + q] = done
-        flight[g] = []
-        for d in range(1, 8):
-            place = first * T + core * (n // 2 * T) + my_x * q
-            copy = remote(
-                u3.at[:, pl.ds(fine_at, q)], full.at[:, ds(place, q)],
-                s4.at[g, d - 1], q4.at[g, d - 1], ((sec + d) % 8, me),
-            )
+
+        def place_of(source):
+            return first * T + source % 2 * (n // 2 * T) + source // 2 * q
+
+        gathering[g] = []
+        for d in range(1, 8) if everyone else (1, 2, 3):
+            copy = copy_of(d, sec)
             copy.start()
             sends.append(copy)
-            src = (sec + 8 - d) % 8
-            place = first * T + (src % 2) * (n // 2 * T) + (src // 2) * q
-            flight[g].append(
-                remote(
-                    u3.at[:, pl.ds(fine_at, q)], full.at[:, ds(place, q)],
-                    s4.at[g, d - 1], q4.at[g, d - 1], ((sec + d) % 8, me),
-                )
-            )
-        full[:, ds(first * T + core * (n // 2 * T) + my_x * q, q)] = done
-
-    def stage_5(g):
-        for copy in flight[g]:
+            gathering[g].append(copy_of(d, (sec + 8 - (d if everyone else 2 * d)) % 8))
+        full[:, ds(place_of(sec), q)] = own[:, at : at + q]
+
+    def share(g):
+        first, n = GROUPS[g]
+        w = n // 2 * T
+        for copy in gathering[g]:
             copy.wait_recv()
+
+        def copy_of(c):
+            where = full.at[:, ds(first * T + c * w, w)]
+            return remote(where, where, s4.at[g, 7], q4.at[g, 7], other_core)
+
+        copy = copy_of(core)
+        copy.start()
+        sends.append(copy)
+        gathering[g] = [copy_of(1 - core)]
 
     l_vol.wait()
     l_cot.wait()
@@ -394,8 +435,6 @@
     lo, hi = arrived(cot_pair, h_cot)
     cots = jnp.concatenate([lo, cot[...], hi], axis=0)
     t7[...] = (cots.astype(F32) * slope(z7)).astype(BF)
-    grad_128(turned(t7[64:192]), window(b_j, 64, 64, T, 3), 54, 27, 3, JOIN_AT)
-    stage_0(0)
     spread(b_s, layers_of(t7))
     back = conv_back(b_s, wj, T, 64)
     e_skip[...] = back[:, T:256]
@@ -404,7 +443,6 @@
     e3 = mm_t(lift_blocks, wu[...]).astype(BF)
     t4[...] = (e3.astype(F32) * slope(z4[16:32])).astype(BF)
     pair = swap(8, t4, t4, h_t4)
-    stage_1(0)
     for t in range(8):
         diag[t * 16 : (t + 1) * 16, t * 256 : (t + 1) * 256] = g2[16:32]
     moved_t = turned(moved)
@@ -413,8 +451,20 @@
         for b in range(8):
             at = UP_AT * T + (b % 4) * 256
             packed[2 * t + b // 4, :, at : at + 256] = up[b * 16 : (b + 1) * 16]
-    grad_256(turned(t4[...]), window(b_c, 16, 16, 16, 2), 54, BOTTOM_AT)
-    stage_0(1)
+    step_t = turned(t4[...])
+    grad_256(step_t, window(b_c, 16, 16, 16, 2), 0, 8, BOTTOM_AT)
+    cross(0)
+    grad_256(step_t, window(b_c, 16, 16, 16, 2), 8, 24, BOTTOM_AT)
+    cross(1)
+    grad_256(step_t, window(b_c, 16, 16, 16, 2), 24, 40, BOTTOM_AT)
+    cross(2)
+    grad_256(step_t, window(b_c, 16, 16, 16, 2), 40, 54, BOTTOM_AT)
+    step_t = turned(t7[64:192])
+    grad_128(step_t, window(b_j, 64, 64, T, 3), 54, 27, 3, JOIN_AT, 0, 3)
+    cross(3)
+    grad_128(step_t, window(b_j, 64, 64, T, 3), 54, 27, 3, JOIN_AT, 3, 27)
+    cross(4)
+    go_on(0)
     lo, hi = arrived(pair, h_t4)
     spread_coarse(b_4, [lo, t4[...], hi])
     e4 = conv_back(b_4, wb, 16, 16).astype(BF)
@@ -425,18 +475,18 @@
     e5 = mm(perm_t[...], high) + mm(perm_t[...], low)
     t2[...] = ((e5 + e_skip[...]) * slope(z2[...])).astype(BF)
     pair = swap(10, t2.at[pl.ds(0, 64)], t2.at[pl.ds(64, 64)], h_t2)
-    stage_1(1)
-    grad_256(turned(t3), lambda n: blocks[32:48, n * T : (n + 2) * T], 8, DOWN_AT)
+    go_on(1, 2, 4, 3)
+    grad_256(turned(t3), lambda n: blocks[32:48, n * T : (n + 2) * T], 0, 8, DOWN_AT)
     grad_128(turned(t2[...]), window(b_1, 256, 64, T, 1), 27, 14, 1, ENC_AT)
-    stage_0(2)
-    stage_2(0)
+    cross(5)
+    go_on(6, 5, 0)
     spread(b_s, layers_of(t2), 64)
     lo, hi = arrived(pair, h_t2)
     spread(b_s, [lo], 0)
     spread(b_s, [hi], 192)
     back = conv_back(b_s, we, T, 64)
     t1 = (back.astype(BF).astype(F32) * slope(z1[...])).astype(BF)
-    stage_1(2)
+    go_on(1)
     for j in range(14):
         left, right = (b_v[320 + t // 9 * 64 : 448 + t // 9 * 64, t % 9 * T : (t % 9 + 1) * T] for t in (2 * j, min(2 * j + 1, 26)))
         tile = left * half_mask[0]
@@ -444,21 +494,31 @@
             tile = tile + right * half_mask[1]
         a_f[:, j * T : (j + 1) * T] = tile
     grad_128(turned(t1), lambda n: a_f[:, n * T : (n + 1) * T], 14, 7, 1, FIRST_AT)
-    stage_0(3)
-    stage_3(0)
-    stage_1(3)
-    stage_4(0)
-    stage_2(1)
-    stage_2(2)
-    stage_2(3)
-    stage_3(1)
-    stage_3(2)
-    stage_3(3)
-    stage_4(1)
-    stage_4(2)
-    stage_4(3)
-    for g, (first, n) in enumerate(GROUPS):
-        stage_5(g)
+    cross(6)
+    go_on(7, 8, 3, 2, 5, 0, 9, 1, 4, 6, 7, 8, 3, 5, 0, 2, 9, 1, 4, 6, 7, 8, 5, 0, 3, 2, 1, 9, 6, 4, 7, 0, 8)
+    gather(0)
+    go_on(5, 2, 1)
+    gather(1)
+    go_on(3, 9, 6, 4)
+    gather(3)
+    go_on(7, 8)
+    gather(5)
+    go_on(2)
+    gather(2)
+    go_on(5, 6)
+    gather(4)
+    go_on(9)
+    gather(6, True)
+    share(0)
+    share(5)
+    share(3)
+    share(1)
+    share(2)
+    share(4)
+    for g in (0, 1, 2, 3, 4, 5, 6):
+        first, n = GROUPS[g]
+        for copy in gathering[g]:
+            copy.wait_recv()
         full_o[:, first * T : (first + n) * T] = full[:, first * T : (first + n) * T]
     for copy in sends:
         copy.wait_send()
@@ -486,6 +546,18 @@
     gf_o[:, 896:1728] = both[8:16, 0:832]
 
 
+def flow_scratch(tiles, how):
+    v, w = lambda *shape: pltpu.VMEM((*shape, 16, tiles * T), BF), (16, 4, 1)
+    two = [how[i] == "b" for i in range(3)]
+    return {
+        "u": [v(4, m) for m in w],
+        "r": [v(2 if two[i] else 3, m) for i, m in enumerate(w)],
+        **{name: [v(m) if two[i] else v(1) for i, m in enumerate(w)] for name in ("keep", "pass", "got")},
+        "send": pltpu.SemaphoreType.DMA((18,)),
+        "recv": pltpu.SemaphoreType.DMA((18,)),
+    }
+
+
 def scratch():
     v, dma = pltpu.VMEM, pltpu.SemaphoreType.DMA
     return [
@@ -497,11 +569,8 @@
         v((T, T), F32), v((T, T), F32), v((T, T), F32),
         v((768, T), BF), v((640, T), BF), v((384, T), BF), v((256, T), BF), v((T, T), BF), v((16, 256), BF),
         v((7, T, 64), BF), v((2, 64, T), BF), v((2, 64, T), BF), v((2, 16, 256), BF), dma((12,)), dma((12,)),
-        v((16, 16, COLS), BF), v((16, 16, HALF), BF), v((4, 4, 16, HALF), BF), v((3, 4, 16, HALF), BF),
-        v((4, 16, HALF), BF), v((3, 16, HALF), BF), v((16, HALF), BF), v((3, 16, EIGHTH), BF), v((16, EIGHTH), BF),
-        v((16, COLS), BF),
-        dma((4,)), dma((4,)), dma((4, 3)), dma((4, 3)), dma((4, 3)), dma((4, 3)), dma((4, 3)), dma((4, 3)),
-        dma((4, 7)), dma((4, 7)),
+        v((16, 16, COLS), BF), v((16, 16, HALF), BF), v((16, EIGHTH), BF), v((16, COLS), BF),
+        dma((8,)), dma((8,)), dma((8, 8)), dma((8, 8)), [flow_scratch(*f[3:]) for f in FLOWS],
     ]
 
 

time: 76 us -> 72.6 us (0.955)
  Pallas kernels: 75.3 us -> 71.8 us
    pallas_call x1, Pallas kernels: 73.3 us -> 69.8 us  [body(): pl.pallas_call(kernel, out_shape=(out((128, 128), BF), out((16, COLS), BF...]
where the time goes in v3:
time: 72.6 us; the launch traced here: 72.4 us
  Pallas kernels  71.8 us (99%)
    pallas_call x1, Pallas kernels, body(): pl.pallas_call(kernel, out_shape=(out((128, 128), BF), out((16, COLS), BF...  69.8 us
    pallas_call x1, Pallas kernels, body(): pl.pallas_call(finish, out_shape=(out((128, 128), BF), out((8, 1728)), ou...  2 us

profile of v3, /device:TPU:1, one launch (start us, length us, event | category | flops | bytes accessed | tf_op | source)
XLA Modules:
  0.0 72.4 jit_solution(8331303673175340830)
XLA Ops:
  0.6 69.8 %step.1 = (bf16[128,128]{1,0:T(8,128)(2,1)}, bf16[16,15360]{1,0:T(8,128)(2,1)}) custom-call(bf16[128,64]{1,0:T(8,128)(2,1)} %bitcast.9, bf16[1728,128]{1,0:T(8,128)(2,1)} %wf_h.1, bf16[3456,128]{1,0:T(8,128)(2,1)} %we_h.1, bf16[1024,256]{1,0:T(8,128)(2,1)} %wd_h.1, bf16[6912,256]{1,0:T(8,128)(2,1)} %wb_h.1, bf16[256,1024]{1,0:T(8,128)(2,1)} %wu_h.1, ...), custom_call_target="tpu_custom_call" | custom-call | tf_op jit(solution)/shard_map/step/pallas_call | solution.py:579
  70.4 2.0 %finish.1 = (bf16[128,128]{1,0:T(8,128)(2,1)}, f32[8,1728]{1,0:T(8,128)}, f32[8,3456]{1,0:T(8,128)}, f32[16,1024]{1,0:T(8,128)}, f32[16,6912]{1,0:T(8,128)}, /*index=5*/f32[64,256]{1,0:T(8,128)}, f32[8,6912]{1,0:T(8,128)}) custom-call(bf16[128,128]{1,0:T(8,128)(2,1)} %get-tuple-element.16.dec, bf16[16,15360]{1,0:T(8,128)(2,1)} %get-tuple-element.17.full), custom_call_target="tpu_custom_call" | custom-call | tf_op jit(solution)/shard_map/finish/pallas_call | solution.py:592

commit v4 on v3

--- a/solution.py
+++ b/solution.py
@@ -19,11 +19,11 @@
 FLOWS = (
     (0, "A", 0, 2, "bbd"),
     (1, "A", 0, 2, "bbd"),
-    (2, "X", 0, 2, "bbd"),
-    (3, "A", 0, 1, "bdd"),
-    (3, "X", 1, 1, "bdd"),
-    (4, "A", 0, 2, "bbd"),
-    (4, "X", 2, 1, "bbd"),
+    (2, "A", 0, 1, "bdd"),
+    (2, "X", 1, 1, "bdd"),
+    (3, "A", 0, 2, "bdd"),
+    (4, "A", 0, 1, "bdd"),
+    (4, "X", 1, 2, "bdd"),
     (5, "A", 0, 2, "bdd"),
     (5, "X", 2, 1, "bdd"),
     (6, "A", 0, 1, "bdd"),
@@ -475,18 +475,17 @@
     e5 = mm(perm_t[...], high) + mm(perm_t[...], low)
     t2[...] = ((e5 + e_skip[...]) * slope(z2[...])).astype(BF)
     pair = swap(10, t2.at[pl.ds(0, 64)], t2.at[pl.ds(64, 64)], h_t2)
-    go_on(1, 2, 4, 3)
+    go_on(1, 3, 2, 4)
     grad_256(turned(t3), lambda n: blocks[32:48, n * T : (n + 2) * T], 0, 8, DOWN_AT)
     grad_128(turned(t2[...]), window(b_1, 256, 64, T, 1), 27, 14, 1, ENC_AT)
     cross(5)
-    go_on(6, 5, 0)
+    go_on(5, 6, 0)
     spread(b_s, layers_of(t2), 64)
     lo, hi = arrived(pair, h_t2)
     spread(b_s, [lo], 0)
     spread(b_s, [hi], 192)
     back = conv_back(b_s, we, T, 64)
     t1 = (back.astype(BF).astype(F32) * slope(z1[...])).astype(BF)
-    go_on(1)
     for j in range(14):
         left, right = (b_v[320 + t // 9 * 64 : 448 + t // 9 * 64, t % 9 * T : (t % 9 + 1) * T] for t in (2 * j, min(2 * j + 1, 26)))
         tile = left * half_mask[0]
@@ -495,25 +494,24 @@
         a_f[:, j * T : (j + 1) * T] = tile
     grad_128(turned(t1), lambda n: a_f[:, n * T : (n + 1) * T], 14, 7, 1, FIRST_AT)
     cross(6)
-    go_on(7, 8, 3, 2, 5, 0, 9, 1, 4, 6, 7, 8, 3, 5, 0, 2, 9, 1, 4, 6, 7, 8, 5, 0, 3, 2, 1, 9, 6, 4, 7, 0, 8)
+    go_on(1, 7, 3, 8, 2, 4, 9, 5, 0, 6, 1, 3, 7, 8, 2, 4, 9, 5, 0, 6, 1, 3, 7, 8, 2, 4, 9, 5, 0, 6, 1, 3, 2, 7, 4)
+    gather(3)
+    go_on(8)
+    gather(2)
+    go_on(9, 5, 0)
     gather(0)
-    go_on(5, 2, 1)
+    go_on(6)
+    gather(4)
+    go_on(1)
     gather(1)
-    go_on(3, 9, 6, 4)
-    gather(3)
     go_on(7, 8)
-    gather(5)
-    go_on(2)
-    gather(2)
-    go_on(5, 6)
-    gather(4)
+    gather(5, True)
+    share(2)
     go_on(9)
     gather(6, True)
+    share(3)
     share(0)
-    share(5)
-    share(3)
     share(1)
-    share(2)
     share(4)
     for g in (0, 1, 2, 3, 4, 5, 6):
         first, n = GROUPS[g]

time: 72.6 us -> 71.7 us (0.988)
  Pallas kernels: 71.8 us -> 70.9 us
    pallas_call x1, Pallas kernels: 69.8 us -> 68.9 us  [body(): pl.pallas_call(kernel, out_shape=(out((128, 128), BF), out((16, COLS), BF...]
where the time goes in v4:
time: 71.7 us; the launch traced here: 71.6 us
  Pallas kernels  70.9 us (99%)
    pallas_call x1, Pallas kernels, body(): pl.pallas_call(kernel, out_shape=(out((128, 128), BF), out((16, COLS), BF...  68.9 us
    pallas_call x1, Pallas kernels, body(): pl.pallas_call(finish, out_shape=(out((128, 128), BF), out((8, 1728)), ou...  2 us

profile of v4, /device:TPU:1, one launch (start us, length us, event | category | flops | bytes accessed | tf_op | source)
XLA Modules:
  0.0 71.6 jit_solution(10207334977750174457)
XLA Ops:
  0.6 68.9 %step.1 = (bf16[128,128]{1,0:T(8,128)(2,1)}, bf16[16,15360]{1,0:T(8,128)(2,1)}) custom-call(bf16[128,64]{1,0:T(8,128)(2,1)} %bitcast.9, bf16[1728,128]{1,0:T(8,128)(2,1)} %wf_h.1, bf16[3456,128]{1,0:T(8,128)(2,1)} %we_h.1, bf16[1024,256]{1,0:T(8,128)(2,1)} %wd_h.1, bf16[6912,256]{1,0:T(8,128)(2,1)} %wb_h.1, bf16[256,1024]{1,0:T(8,128)(2,1)} %wu_h.1, ...), custom_call_target="tpu_custom_call" | custom-call | tf_op jit(solution)/shard_map/step/pallas_call | solution.py:577
  69.6 2.0 %finish.1 = (bf16[128,128]{1,0:T(8,128)(2,1)}, f32[8,1728]{1,0:T(8,128)}, f32[8,3456]{1,0:T(8,128)}, f32[16,1024]{1,0:T(8,128)}, f32[16,6912]{1,0:T(8,128)}, /*index=5*/f32[64,256]{1,0:T(8,128)}, f32[8,6912]{1,0:T(8,128)}) custom-call(bf16[128,128]{1,0:T(8,128)(2,1)} %get-tuple-element.16.dec, bf16[16,15360]{1,0:T(8,128)(2,1)} %get-tuple-element.17.full), custom_call_target="tpu_custom_call" | custom-call | tf_op jit(solution)/shard_map/finish/pallas_call | solution.py:590

commit v5 on v4

--- a/solution.py
+++ b/solution.py
@@ -69,7 +69,7 @@
     dec_o, full_o,
     vol, wf, we, wd, wb, wu, wj, cot, load_sem,
     shift, shift_c, perm, perm_t, eye, half_mask,
-    wx, b_v, b_1, b_j, b_s, b_c, b_4, a_f, blocks, diag,
+    pairs, b_d, wx, b_v, b_1, b_j, b_s, b_c, b_4, a_f, blocks, diag,
     z1, z2, e_skip,
     h1, sk, li, t7, t2, t4,
     h_vol, h_cot, h_t2, h_t4, h_send, h_recv,
@@ -105,6 +105,15 @@
     for k in range(9):
         oy, oz = k // 3 - 1, k % 3 - 1
         shift[k] = one_hot(((c >> 3) == (r >> 3) + oy) & ((c & 7) == (r & 7) + oz))
+    r, c = iotas((64, T))
+    for j in range(5):
+        hit = None
+        for half in range(2 if j < 4 else 1):
+            oy, oz = (2 * j + half) // 3 - 1, (2 * j + half) % 3 - 1
+            v = c - 64 * half
+            here = (v >= 0) & (v < 64) & ((v >> 3) == (r >> 3) + oy) & ((v & 7) == (r & 7) + oz)
+            hit = here if hit is None else hit | here
+        pairs[j] = one_hot(hit)
     r, c = iotas((16, 16))
     for k in range(9):
         oy, oz = k // 3 - 1, k % 3 - 1
@@ -161,6 +170,17 @@
                     to[row + (n + m) * 64 : row + (n + m + 1) * 64, k * width : (k + 1) * width] = (
                         moved[:, m * width : (m + 1) * width]
                     )
+
+    def spread_narrow(to, layers, row):
+        for n in range(0, len(layers), 2):
+            both = jnp.concatenate(
+                [jnp.concatenate([x * half_mask[0, 0:64], x * half_mask[1, 0:64]], axis=0) for x in layers[n : n + 2]],
+                axis=1,
+            )
+            for j in range(5):
+                moved = mm(pairs[j], both).astype(BF)
+                for m in range(2):
+                    to[row + (n + m) * 64 : row + (n + m + 1) * 64, j * T : (j + 1) * T] = moved[:, m * T : (m + 1) * T]
 
     def layers_of(x):
         return [x[i : i + 64] for i in range(0, x.shape[0], 64)]
@@ -393,14 +413,15 @@
     twice = one_hot(r == (c & 63))
     l_wf.wait()
     zero = jnp.zeros((64, T), BF)
-    for tap in range(27):
-        wx[tap * T : tap * T + 64, :] = wf[tap * 64 : (tap + 1) * 64, :]
-        wx[tap * T + 64 : (tap + 1) * T, :] = zero
-    spread(b_v, layers_of(mm(vol[...], twice).astype(BF)), 6 * 64)
+    for ox in range(3):
+        wx[ox * 640 : ox * 640 + 576, :] = wf[ox * 576 : (ox + 1) * 576, :]
+        wx[ox * 640 + 576 : (ox + 1) * 640, :] = zero
+    own_layers = layers_of(mm(vol[...], twice).astype(BF))
+    spread_narrow(b_v, own_layers, 6 * 64)
     for d in (-1, 1, -2, 2, -3, 3):
         pushed[d].wait_recv()
         got = inside(mm(h_vol[3 + d], twice), 2 * (me + d), 32, 64)
-        spread(b_v, layers_of(got), (3 + d) * T)
+        spread_narrow(b_v, layers_of(got), (3 + d) * T)
     z1_all = conv(b_v, wx, 768, 64)
     z1[...] = z1_all[320:448]
     h1[...] = inside(silu(z1_all), 2 * me - 5, 32, 64)
@@ -465,6 +486,9 @@
     grad_128(step_t, window(b_j, 64, 64, T, 3), 54, 27, 3, JOIN_AT, 3, 27)
     cross(4)
     go_on(0)
+    before_own = inside(mm(h_vol[2], twice), 2 * (me - 1), 32, 64)
+    after_own = inside(mm(h_vol[4], twice), 2 * (me + 1), 32, 64)
+    spread(b_d, [before_own[64:128], *layers_of(mm(vol[...], twice).astype(BF)), after_own[0:64]])
     lo, hi = arrived(pair, h_t4)
     spread_coarse(b_4, [lo, t4[...], hi])
     e4 = conv_back(b_4, wb, 16, 16).astype(BF)
@@ -487,7 +511,7 @@
     back = conv_back(b_s, we, T, 64)
     t1 = (back.astype(BF).astype(F32) * slope(z1[...])).astype(BF)
     for j in range(14):
-        left, right = (b_v[320 + t // 9 * 64 : 448 + t // 9 * 64, t % 9 * T : (t % 9 + 1) * T] for t in (2 * j, min(2 * j + 1, 26)))
+        left, right = (b_d[t // 9 * 64 : 128 + t // 9 * 64, t % 9 * T : (t % 9 + 1) * T] for t in (2 * j, min(2 * j + 1, 26)))
         tile = left * half_mask[0]
         if j < 13:
             tile = tile + right * half_mask[1]
@@ -562,7 +586,7 @@
         v((128, 64), BF), v((1728, 128), BF), v((3456, 128), BF), v((1024, 256), BF), v((6912, 256), BF),
         v((256, 1024), BF), v((6912, 128), BF), v((128, 128), BF), dma((8,)),
         v((9, 64, 64), BF), v((144, 16), BF), v((T, T), BF), v((T, T), BF), v((256, 256), BF), v((2, T, T), BF),
-        v((3456, T), BF), v((896, 1152), BF), v((768, 1152), BF), v((384, 2304), BF), v((256, 1152), BF),
+        v((5, 64, T), BF), v((256, 1152), BF), v((1920, T), BF), v((896, 640), BF), v((768, 1152), BF), v((384, 2304), BF), v((256, 1152), BF),
         v((80, 2304), BF), v((48, 2304), BF), v((T, 1792), BF), v((80, 1024), BF), v((T, 2048), BF),
         v((T, T), F32), v((T, T), F32), v((T, T), F32),
         v((768, T), BF), v((640, T), BF), v((384, T), BF), v((256, T), BF), v((T, T), BF), v((16, 256), BF),

time: 71.7 us -> 70.2 us (0.979)
  Pallas kernels: 70.9 us -> 69.4 us
    pallas_call x1, Pallas kernels: 68.9 us -> 67.4 us  [body(): pl.pallas_call(kernel, out_shape=(out((128, 128), BF), out((16, COLS), BF...]
where the time goes in v5:
time: 70.2 us; the launch traced here: 70.1 us
  Pallas kernels  69.4 us (99%)
    pallas_call x1, Pallas kernels, body(): pl.pallas_call(kernel, out_shape=(out((128, 128), BF), out((16, COLS), BF...  67.4 us
    pallas_call x1, Pallas kernels, body(): pl.pallas_call(finish, out_shape=(out((128, 128), BF), out((8, 1728)), ou...  2 us

profile of v5, /device:TPU:1, one launch (start us, length us, event | category | flops | bytes accessed | tf_op | source)
XLA Modules:
  0.0 70.1 jit_solution(4456204099549610226)
XLA Ops:
  0.6 67.4 %step.1 = (bf16[128,128]{1,0:T(8,128)(2,1)}, bf16[16,15360]{1,0:T(8,128)(2,1)}) custom-call(bf16[128,64]{1,0:T(8,128)(2,1)} %bitcast.9, bf16[1728,128]{1,0:T(8,128)(2,1)} %wf_h.1, bf16[3456,128]{1,0:T(8,128)(2,1)} %we_h.1, bf16[1024,256]{1,0:T(8,128)(2,1)} %wd_h.1, bf16[6912,256]{1,0:T(8,128)(2,1)} %wb_h.1, bf16[256,1024]{1,0:T(8,128)(2,1)} %wu_h.1, ...), custom_call_target="tpu_custom_call" | custom-call | tf_op jit(solution)/shard_map/step/pallas_call | solution.py:601
  68.1 2.0 %finish.1 = (bf16[128,128]{1,0:T(8,128)(2,1)}, f32[8,1728]{1,0:T(8,128)}, f32[8,3456]{1,0:T(8,128)}, f32[16,1024]{1,0:T(8,128)}, f32[16,6912]{1,0:T(8,128)}, /*index=5*/f32[64,256]{1,0:T(8,128)}, f32[8,6912]{1,0:T(8,128)}) custom-call(bf16[128,128]{1,0:T(8,128)(2,1)} %get-tuple-element.16.dec, bf16[16,15360]{1,0:T(8,128)(2,1)} %get-tuple-element.17.full), custom_call_target="tpu_custom_call" | custom-call | tf_op jit(solution)/shard_map/finish/pallas_call | solution.py:614

commit v6 on v5

--- a/solution.py
+++ b/solution.py
@@ -18,15 +18,14 @@
 HALF, EIGHTH = COLS // 2, COLS // 8
 FLOWS = (
     (0, "A", 0, 2, "bbd"),
-    (1, "A", 0, 2, "bbd"),
-    (2, "A", 0, 1, "bdd"),
-    (2, "X", 1, 1, "bdd"),
-    (3, "A", 0, 2, "bdd"),
-    (4, "A", 0, 1, "bdd"),
-    (4, "X", 1, 2, "bdd"),
+    (1, "A", 0, 2, "bdd"),
+    (2, "X", 0, 2, "bdd"),
+    (3, "A", 0, 1, "bdd"),
+    (3, "X", 1, 1, "bdd"),
+    (4, "A", 0, 3, "bdd"),
     (5, "A", 0, 2, "bdd"),
     (5, "X", 2, 1, "bdd"),
-    (6, "A", 0, 1, "bdd"),
+    (6, "X", 0, 1, "bdd"),
 )
 
 
@@ -406,7 +405,7 @@
     l_cot.wait()
     pl.semaphore_wait(barrier, len(peers))
     pushed = {}
-    for n, d in enumerate((1, -1, 2, -2, 3, -3)):
+    for n, d in enumerate((3, -3, 2, -2, 1, -1)):
         pushed[-d] = push(n, vol, h_vol.at[3 - d], around[d])
     cot_pair = swap(6, cot.at[pl.ds(0, 64)], cot.at[pl.ds(64, 64)], h_cot)
     r, c = iotas((64, T))
@@ -418,6 +417,7 @@
         wx[ox * 640 + 576 : (ox + 1) * 640, :] = zero
     own_layers = layers_of(mm(vol[...], twice).astype(BF))
     spread_narrow(b_v, own_layers, 6 * 64)
+    spread(b_d, own_layers, 64)
     for d in (-1, 1, -2, 2, -3, 3):
         pushed[d].wait_recv()
         got = inside(mm(h_vol[3 + d], twice), 2 * (me + d), 32, 64)
@@ -486,9 +486,6 @@
     grad_128(step_t, window(b_j, 64, 64, T, 3), 54, 27, 3, JOIN_AT, 3, 27)
     cross(4)
     go_on(0)
-    before_own = inside(mm(h_vol[2], twice), 2 * (me - 1), 32, 64)
-    after_own = inside(mm(h_vol[4], twice), 2 * (me + 1), 32, 64)
-    spread(b_d, [before_own[64:128], *layers_of(mm(vol[...], twice).astype(BF)), after_own[0:64]])
     lo, hi = arrived(pair, h_t4)
     spread_coarse(b_4, [lo, t4[...], hi])
     e4 = conv_back(b_4, wb, 16, 16).astype(BF)
@@ -499,12 +496,17 @@
     e5 = mm(perm_t[...], high) + mm(perm_t[...], low)
     t2[...] = ((e5 + e_skip[...]) * slope(z2[...])).astype(BF)
     pair = swap(10, t2.at[pl.ds(0, 64)], t2.at[pl.ds(64, 64)], h_t2)
-    go_on(1, 3, 2, 4)
+    go_on(1, 2, 4, 3)
     grad_256(turned(t3), lambda n: blocks[32:48, n * T : (n + 2) * T], 0, 8, DOWN_AT)
     grad_128(turned(t2[...]), window(b_1, 256, 64, T, 1), 27, 14, 1, ENC_AT)
     cross(5)
-    go_on(5, 6, 0)
+    go_on(5)
     spread(b_s, layers_of(t2), 64)
+    go_on(0)
+    before_own = inside(mm(h_vol[2], twice), 2 * (me - 1), 32, 64)
+    after_own = inside(mm(h_vol[4], twice), 2 * (me + 1), 32, 64)
+    spread(b_d, [before_own[64:128]], 0)
+    spread(b_d, [after_own[0:64]], 192)
     lo, hi = arrived(pair, h_t2)
     spread(b_s, [lo], 0)
     spread(b_s, [hi], 192)
@@ -518,24 +520,24 @@
         a_f[:, j * T : (j + 1) * T] = tile
     grad_128(turned(t1), lambda n: a_f[:, n * T : (n + 1) * T], 14, 7, 1, FIRST_AT)
     cross(6)
-    go_on(1, 7, 3, 8, 2, 4, 9, 5, 0, 6, 1, 3, 7, 8, 2, 4, 9, 5, 0, 6, 1, 3, 7, 8, 2, 4, 9, 5, 0, 6, 1, 3, 2, 7, 4)
+    go_on(1, 6, 7, 3, 2, 8, 4, 5, 0, 1, 6, 7, 3, 2, 0, 5, 8, 1, 4, 6, 7, 3, 0, 2, 8, 1)
+    gather(1)
+    go_on(5, 4, 3, 6, 7, 0)
+    gather(0)
+    go_on(2)
+    gather(2)
+    go_on(8, 4)
     gather(3)
+    share(1)
+    go_on(5)
+    gather(4)
+    go_on(6, 7)
+    gather(5, True)
     go_on(8)
-    gather(2)
-    go_on(9, 5, 0)
-    gather(0)
-    go_on(6)
-    gather(4)
-    go_on(1)
-    gather(1)
-    go_on(7, 8)
-    gather(5, True)
+    gather(6, True)
     share(2)
-    go_on(9)
-    gather(6, True)
     share(3)
     share(0)
-    share(1)
     share(4)
     for g in (0, 1, 2, 3, 4, 5, 6):
         first, n = GROUPS[g]

time: 70.2 us -> 70.6 us (level)
  no operation moved by 1% of the time
where the time goes in v6:
time: 70.6 us; the launch traced here: 70.4 us
  Pallas kernels  69.8 us (99%)
    pallas_call x1, Pallas kernels, body(): pl.pallas_call(kernel, out_shape=(out((128, 128), BF), out((16, COLS), BF...  67.8 us
    pallas_call x1, Pallas kernels, body(): pl.pallas_call(finish, out_shape=(out((128, 128), BF), out((8, 1728)), ou...  2 us

profile of v6, /device:TPU:1, one launch (start us, length us, event | category | flops | bytes accessed | tf_op | source)
XLA Modules:
  0.0 70.4 jit_solution(5700909471027541351)
XLA Ops:
  0.6 67.8 %step.1 = (bf16[128,128]{1,0:T(8,128)(2,1)}, bf16[16,15360]{1,0:T(8,128)(2,1)}) custom-call(bf16[128,64]{1,0:T(8,128)(2,1)} %bitcast.9, bf16[1728,128]{1,0:T(8,128)(2,1)} %wf_h.1, bf16[3456,128]{1,0:T(8,128)(2,1)} %we_h.1, bf16[1024,256]{1,0:T(8,128)(2,1)} %wd_h.1, bf16[6912,256]{1,0:T(8,128)(2,1)} %wb_h.1, bf16[256,1024]{1,0:T(8,128)(2,1)} %wu_h.1, ...), custom_call_target="tpu_custom_call" | custom-call | tf_op jit(solution)/shard_map/step/pallas_call | solution.py:603
  68.4 2.0 %finish.1 = (bf16[128,128]{1,0:T(8,128)(2,1)}, f32[8,1728]{1,0:T(8,128)}, f32[8,3456]{1,0:T(8,128)}, f32[16,1024]{1,0:T(8,128)}, f32[16,6912]{1,0:T(8,128)}, /*index=5*/f32[64,256]{1,0:T(8,128)}, f32[8,6912]{1,0:T(8,128)}) custom-call(bf16[128,128]{1,0:T(8,128)(2,1)} %get-tuple-element.16.dec, bf16[16,15360]{1,0:T(8,128)(2,1)} %get-tuple-element.17.full), custom_call_target="tpu_custom_call" | custom-call | tf_op jit(solution)/shard_map/finish/pallas_call | solution.py:616

commit v7 on v5

--- a/solution.py
+++ b/solution.py
@@ -406,7 +406,7 @@
     l_cot.wait()
     pl.semaphore_wait(barrier, len(peers))
     pushed = {}
-    for n, d in enumerate((1, -1, 2, -2, 3, -3)):
+    for n, d in enumerate((3, -3, 2, -2, 1, -1)):
         pushed[-d] = push(n, vol, h_vol.at[3 - d], around[d])
     cot_pair = swap(6, cot.at[pl.ds(0, 64)], cot.at[pl.ds(64, 64)], h_cot)
     r, c = iotas((64, T))
@@ -418,6 +418,7 @@
         wx[ox * 640 + 576 : (ox + 1) * 640, :] = zero
     own_layers = layers_of(mm(vol[...], twice).astype(BF))
     spread_narrow(b_v, own_layers, 6 * 64)
+    spread(b_d, own_layers, 64)
     for d in (-1, 1, -2, 2, -3, 3):
         pushed[d].wait_recv()
         got = inside(mm(h_vol[3 + d], twice), 2 * (me + d), 32, 64)
@@ -486,9 +487,6 @@
     grad_128(step_t, window(b_j, 64, 64, T, 3), 54, 27, 3, JOIN_AT, 3, 27)
     cross(4)
     go_on(0)
-    before_own = inside(mm(h_vol[2], twice), 2 * (me - 1), 32, 64)
-    after_own = inside(mm(h_vol[4], twice), 2 * (me + 1), 32, 64)
-    spread(b_d, [before_own[64:128], *layers_of(mm(vol[...], twice).astype(BF)), after_own[0:64]])
     lo, hi = arrived(pair, h_t4)
     spread_coarse(b_4, [lo, t4[...], hi])
     e4 = conv_back(b_4, wb, 16, 16).astype(BF)
@@ -505,6 +503,10 @@
     cross(5)
     go_on(5, 6, 0)
     spread(b_s, layers_of(t2), 64)
+    before_own = inside(mm(h_vol[2], twice), 2 * (me - 1), 32, 64)
+    after_own = inside(mm(h_vol[4], twice), 2 * (me + 1), 32, 64)
+    spread(b_d, [before_own[64:128]], 0)
+    spread(b_d, [after_own[0:64]], 192)
     lo, hi = arrived(pair, h_t2)
     spread(b_s, [lo], 0)
     spread(b_s, [hi], 192)

time: 70.2 us -> 71.3 us (1.016)
  Pallas kernels: 69.4 us -> 70.6 us
    pallas_call x1, Pallas kernels: 67.4 us -> 68.6 us  [body(): pl.pallas_call(kernel, out_shape=(out((128, 128), BF), out((16, COLS), BF...]
where the time goes in v7:
time: 71.3 us; the launch traced here: 71.2 us
  Pallas kernels  70.6 us (99%)
    pallas_call x1, Pallas kernels, body(): pl.pallas_call(kernel, out_shape=(out((128, 128), BF), out((16, COLS), BF...  68.6 us
    pallas_call x1, Pallas kernels, body(): pl.pallas_call(finish, out_shape=(out((128, 128), BF), out((8, 1728)), ou...  2 us

profile of v7, /device:TPU:1, one launch (start us, length us, event | category | flops | bytes accessed | tf_op | source)
XLA Modules:
  0.0 71.2 jit_solution(17553812034994439713)
XLA Ops:
  0.6 68.6 %step.1 = (bf16[128,128]{1,0:T(8,128)(2,1)}, bf16[16,15360]{1,0:T(8,128)(2,1)}) custom-call(bf16[128,64]{1,0:T(8,128)(2,1)} %bitcast.9, bf16[1728,128]{1,0:T(8,128)(2,1)} %wf_h.1, bf16[3456,128]{1,0:T(8,128)(2,1)} %we_h.1, bf16[1024,256]{1,0:T(8,128)(2,1)} %wd_h.1, bf16[6912,256]{1,0:T(8,128)(2,1)} %wb_h.1, bf16[256,1024]{1,0:T(8,128)(2,1)} %wu_h.1, ...), custom_call_target="tpu_custom_call" | custom-call | tf_op jit(solution)/shard_map/step/pallas_call | solution.py:603
  69.2 2.0 %finish.1 = (bf16[128,128]{1,0:T(8,128)(2,1)}, f32[8,1728]{1,0:T(8,128)}, f32[8,3456]{1,0:T(8,128)}, f32[16,1024]{1,0:T(8,128)}, f32[16,6912]{1,0:T(8,128)}, /*index=5*/f32[64,256]{1,0:T(8,128)}, f32[8,6912]{1,0:T(8,128)}) custom-call(bf16[128,128]{1,0:T(8,128)(2,1)} %get-tuple-element.16.dec, bf16[16,15360]{1,0:T(8,128)(2,1)} %get-tuple-element.17.full), custom_call_target="tpu_custom_call" | custom-call | tf_op jit(solution)/shard_map/finish/pallas_call | solution.py:616
